TPU v7x, 32 devices: a whole 2x2x4 slice. The times are simulated.
32 devices in a mesh: dp: 2 (over core), mp: 4 (over y, x), hidden: 4 (over z).
Axes of the slice: x: 2, y: 2, z: 4, core: 2. Of those that a mesh axis runs over, the one named last changes fastest.
Arguments:
- stored: bfloat16 [768, 32768], P('mp', ('dp', 'hidden')), may hold values from -51 to 51
- positions: int32 [32768], P(('dp', 'hidden')), may hold values from 0 to 1211, as said below
- segments: int32 [32768], P(('dp', 'hidden', 'mp')), may hold values from 0 to 8, as said below
- present: int32 [32768], P(('dp', 'hidden', 'mp')), may hold values from 0 to 1, as said below
- norm_gains: float32 [2, 768], P(None, 'mp'), may hold values from 0.1 to 1.9
- norm_biases: float32 [2, 768], P(None, 'mp'), may hold values from -3 to 3
- input_proj: bfloat16 [768, 3, 768], P('mp', None, 'hidden'), may hold values from -0.3125 to 0.3125
- input_bias: bfloat16 [2, 768], P(None, 'hidden'), may hold values from -3 to 3
- output_proj: bfloat16 [768, 768], P('hidden', 'mp'), may hold values from -0.875 to 0.875
- output_bias: bfloat16 [768], P('mp'), may hold values from -3 to 3
- expand_weight: bfloat16 [768, 3072], P('mp', 'hidden'), may hold values from -0.21875 to 0.21875
- expand_bias: bfloat16 [3072], P('hidden'), may hold values from -3 to 3
- reduce_weight: bfloat16 [768, 3072], P('mp', 'hidden'), may hold values from -0.109375 to 0.109375
- reduce_bias: bfloat16 [768], P('mp'), may hold values from -3 to 3
- cotangent: bfloat16 [768, 32768], P('mp', ('dp', 'hidden')), may hold values from -6 to 6
Outputs:
- output: bfloat16 [768, 32768], P('mp', ('dp', 'hidden'))
- d_stored: float32 [768, 32768], P('mp', ('dp', 'hidden'))
- d_norm_gains: float32 [2, 768], P(None, ('mp', 'dp', 'hidden'))
- d_norm_biases: float32 [2, 768], P(None, ('mp', 'dp', 'hidden'))
- d_input_proj: float32 [768, 3, 768], P(('mp', 'dp'), None, 'hidden')
- d_input_bias: float32 [2, 768], P(None, ('hidden', 'dp'))
- d_output_proj: float32 [768, 768], P(('hidden', 'dp'), 'mp')
- d_output_bias: float32 [768], P(('mp', 'dp'))
- d_expand_weight: float32 [768, 3072], P(('mp', 'dp'), 'hidden')
- d_expand_bias: float32 [3072], P(('hidden', 'dp'))
- d_reduce_weight: float32 [768, 3072], P(('mp', 'dp'), 'hidden')
- d_reduce_bias: float32 [768], P(('mp', 'dp'))
Inputs may be any that keep to these rules, and one draw needn't show every extreme that they name: `segments`: within each packed row of 1024 tokens the clip numbers never fall; every clip but the last of a row holds 128 to 512 tokens; padding tokens carry 8. `present`: padding is the tail of every packed row, 1 to 128 tokens. `positions`: consecutive within a clip; a clip's positions stay below 1212; padding tokens carry 1212 - 1.
All inputs are finite; a program needn't handle non-finite values.
Results may differ from a plain program's by a relative error of at most 0.014.
The roundings to bfloat16 on the way count: a program that leaves them out, or rounds other values in their place, can miss the bound.
Values may be sent and summed in bfloat16 or wider, within the bound.
A program may use at most 384 MiB of HBM per device.

v0:
```python
import math

import jax
import jax.numpy as jnp
from jax import lax
from jax.sharding import PartitionSpec as P

D = 768
HEADS = 12
HD = 64
SEQ = 1024
QBLOCK = 512


norm_eps = 1e-06
masked_score = -1e30


def feature_sums(left_terms, right_terms):
    return lax.psum((jnp.sum(left_terms, axis=1), jnp.sum(right_terms, axis=1)), "mp")


def layer_norm(values, gain_row, shift_row):
    totals, squares = feature_sums(values, values * values)
    average = (totals / D)[:, None]
    spread = (squares / D)[:, None] - average * average
    inv_spread = lax.rsqrt(spread + norm_eps)
    normed = (values - average) * inv_spread
    return (normed * gain_row + shift_row, normed, inv_spread)


def norm_back(grads, normed, inv_spread, gain_row):
    scaled = grads * gain_row
    totals, crossed = feature_sums(scaled, scaled * normed)
    return inv_spread * (scaled - (totals / D)[:, None] - normed * (crossed / D)[:, None])


def position_table(positions, col_width):
    columns = lax.axis_index("mp") * col_width + jnp.arange(col_width, dtype=jnp.int32)
    half_width = D // 2
    freq_rates = jnp.exp(
        (columns % half_width).astype(jnp.float32) * (-math.log(10000.0) / half_width)
    )
    angles = positions.astype(jnp.float32)[:, None] * freq_rates[None, :]
    return jnp.where(columns[None, :] < half_width, jnp.sin(angles), jnp.cos(angles))


def gelu_slope(values):
    normal_cdf = 0.5 * (1.0 + lax.erf(values * (1.0 / math.sqrt(2.0))))
    return normal_cdf + values * jnp.exp(-0.5 * values * values) * (1.0 / math.sqrt(2.0 * math.pi))


def regroup(values, outer, inner):
    shape = values.shape
    return jnp.swapaxes(values.reshape((outer, inner, -1) + shape[1:]), 0, 1).reshape(shape)


def rows_hidden(values):
    return lax.all_gather(values, "hidden", axis=0, tiled=True)


def rows_model(values):
    return lax.all_gather(values, "mp", axis=0, tiled=True)


def sum_model(partial_term, row_total):
    return lax.psum_scatter(
        partial_term(jnp.int32(0), row_total * lax.axis_size("mp")),
        "mp",
        scatter_dimension=0,
        tiled=True,
    )


def sum_hidden(partial_term, row_total):
    return lax.psum_scatter(
        partial_term(jnp.int32(0), row_total * lax.axis_size("hidden")),
        "hidden",
        scatter_dimension=0,
        tiled=True,
    )


def into_heads(values):
    return lax.all_to_all(values, "hidden", split_axis=0, concat_axis=2, tiled=True)


def from_heads(values):
    return lax.all_to_all(values, "hidden", split_axis=2, concat_axis=0, tiled=True)


def row_product(source, weight, contract):

    def partial_term(row_start, row_count):
        return lax.dot_general(
            source, weight, (((1,), (contract,)), ((), ())), preferred_element_type=jnp.float32
        )

    return partial_term


def block_mask(seg_row, present_row, row_start):
    query_seg = lax.dynamic_slice_in_dim(seg_row, row_start, QBLOCK)
    query_place = row_start + jnp.arange(QBLOCK, dtype=jnp.int32)
    key_place = jnp.arange(SEQ, dtype=jnp.int32)
    same_clip = (query_seg[:, None] == seg_row[None, :]) & (present_row[None, :] == 1)
    return same_clip | (query_place[:, None] == key_place[None, :])


def block_scores(queries, key_rows, mask_rows):
    scores = jnp.einsum(
        "qhd,khd->hqk", queries, key_rows, preferred_element_type=jnp.float32
    ) * HD ** (-0.5)
    return jnp.where(mask_rows[None], scores, masked_score)


def attend_rows(head_layout, segments, present):
    row_total = head_layout.shape[0] // SEQ
    block_total = SEQ // QBLOCK
    head_grid = head_layout.reshape(row_total, SEQ, 3, HEADS, HD)

    def one_row(packed):
        row_data, seg_row, present_row = packed
        query_rows = row_data[:, 0]
        key_rows = row_data[:, 1]
        value_rows = row_data[:, 2]

        def one_block(block_index):
            row_start = block_index * QBLOCK
            queries = lax.dynamic_slice_in_dim(query_rows, row_start, QBLOCK)
            scores = block_scores(queries, key_rows, block_mask(seg_row, present_row, row_start))
            row_max = jnp.max(scores, axis=2, keepdims=True)
            weights = jnp.exp(scores - row_max)
            totals = jnp.sum(weights, axis=2, keepdims=True)
            weights_low = (weights / totals).astype(jnp.bfloat16)
            block_out = jnp.einsum(
                "hqk,khd->qhd", weights_low, value_rows, preferred_element_type=jnp.float32
            )
            return (block_out, row_max[:, :, 0] + jnp.log(totals[:, :, 0]))

        block_outs, log_sums = lax.map(one_block, jnp.arange(block_total, dtype=jnp.int32))
        return (block_outs.reshape(SEQ, HEADS * HD), log_sums)

    row_outs, log_sums = lax.map(
        one_row, (head_grid, segments.reshape(row_total, SEQ), present.reshape(row_total, SEQ))
    )
    return (row_outs.reshape(row_total * SEQ, HEADS * HD), log_sums)


def attend_back(head_layout, out_grads, log_sums, segments, present):
    row_total = head_layout.shape[0] // SEQ
    block_total = SEQ // QBLOCK
    head_grid = head_layout.reshape(row_total, SEQ, 3, HEADS, HD)
    grad_grid = out_grads.reshape(row_total, SEQ, HEADS, HD)

    def one_row(packed):
        row_data, grad_row, sum_row, seg_row, present_row = packed
        query_rows = row_data[:, 0]
        key_rows = row_data[:, 1]
        value_rows = row_data[:, 2]

        def one_block(carry, block_index):
            key_grad, value_grad = carry
            row_start = block_index * QBLOCK
            queries = lax.dynamic_slice_in_dim(query_rows, row_start, QBLOCK)
            block_grad = lax.dynamic_slice_in_dim(grad_row, row_start, QBLOCK)
            scores = block_scores(queries, key_rows, block_mask(seg_row, present_row, row_start))
            soft_rows = jnp.exp(scores - sum_row[block_index][:, :, None])
            prob_grad = jnp.einsum(
                "qhd,khd->hqk", block_grad, value_rows, preferred_element_type=jnp.float32
            )
            inner_sums = jnp.sum(soft_rows * prob_grad, axis=2, keepdims=True)
            score_grad = (soft_rows * (prob_grad - inner_sums)).astype(jnp.bfloat16)
            query_grad = jnp.einsum(
                "hqk,khd->qhd", score_grad, key_rows, preferred_element_type=jnp.float32
            ) * HD ** (-0.5)
            key_grad = key_grad + jnp.einsum(
                "hqk,qhd->khd", score_grad, queries, preferred_element_type=jnp.float32
            ) * HD ** (-0.5)
            value_grad = value_grad + jnp.einsum(
                "hqk,qhd->khd",
                soft_rows.astype(jnp.bfloat16),
                block_grad,
                preferred_element_type=jnp.float32,
            )
            return ((key_grad, value_grad), query_grad)

        zero_rows = jnp.zeros((SEQ, HEADS, HD), jnp.float32)
        (key_grad, value_grad), query_grad = lax.scan(
            one_block, (zero_rows, zero_rows), jnp.arange(block_total, dtype=jnp.int32)
        )
        return jnp.stack([query_grad.reshape(SEQ, HEADS, HD), key_grad, value_grad], axis=1)

    result = lax.map(
        one_row,
        (
            head_grid,
            grad_grid,
            log_sums,
            segments.reshape(row_total, SEQ),
            present.reshape(row_total, SEQ),
        ),
    )
    return result.reshape(row_total * SEQ, 3, HEADS * HD)


def forward(stored_rows, positions, segments, present, params):
    (
        norm_gains,
        norm_biases,
        input_proj,
        input_bias,
        output_proj,
        output_bias,
        expand_weight,
        expand_bias,
        reduce_weight,
        reduce_bias,
    ) = params
    model_size = lax.axis_size("mp")
    hidden_size = lax.axis_size("hidden")
    norm_rows = stored_rows.shape[0]
    split_rows = norm_rows * hidden_size // model_size
    embedded = stored_rows.astype(jnp.float32) + position_table(positions, stored_rows.shape[1])
    first_norm, first_normed, first_scale = layer_norm(embedded, norm_gains[0], norm_biases[0])
    first_low = first_norm.astype(jnp.bfloat16)
    first_rows = regroup(rows_hidden(first_low), hidden_size, model_size)
    flat_input = input_proj.reshape(input_proj.shape[0], -1)
    qkv_sums = sum_model(row_product(first_rows, flat_input, 0), split_rows)
    bias_rows = jnp.stack([input_bias[0], jnp.zeros_like(input_bias[0]), input_bias[1]]).astype(
        jnp.float32
    )
    qkv_low = (qkv_sums.reshape(split_rows, 3, -1) + bias_rows).astype(jnp.bfloat16)
    head_layout = into_heads(qkv_low)
    attended, log_sums = attend_rows(head_layout, segments, present)
    att_cols = from_heads(attended.astype(jnp.bfloat16).reshape(attended.shape[0], 1, -1)).reshape(
        split_rows, -1
    )
    att_rows = regroup(rows_model(att_cols), model_size, hidden_size)
    branch = sum_hidden(row_product(att_rows, output_proj, 0), norm_rows) + output_bias.astype(
        jnp.float32
    )
    middle = embedded + branch
    second_norm, second_normed, second_scale = layer_norm(middle, norm_gains[1], norm_biases[1])
    second_low = second_norm.astype(jnp.bfloat16)
    second_rows = rows_hidden(second_low)
    pre_act = sum_model(
        row_product(second_rows, expand_weight, 0), split_rows
    ) + expand_bias.astype(jnp.float32)
    act_rows = rows_model(jax.nn.gelu(pre_act, approximate=False).astype(jnp.bfloat16))
    mlp_out = sum_hidden(row_product(act_rows, reduce_weight, 1), norm_rows) + reduce_bias.astype(
        jnp.float32
    )
    feed_values = {"tokens": second_rows, "pre_act": pre_act, "act_low": act_rows}
    return {
        "output": middle + mlp_out,
        "first_normed": first_normed,
        "first_scale": first_scale,
        "first_rows": first_rows,
        "head_layout": head_layout,
        "log_sums": log_sums,
        "att_rows": att_rows,
        "attn_full": None,
        "second_normed": second_normed,
        "second_scale": second_scale,
        "feed_values": feed_values,
    }


def local(
    stored,
    positions,
    segments,
    present,
    norm_gains,
    norm_biases,
    input_proj,
    input_bias,
    output_proj,
    output_bias,
    expand_weight,
    expand_bias,
    reduce_weight,
    reduce_bias,
    cotangent,
):
    params = (
        norm_gains,
        norm_biases,
        input_proj,
        input_bias,
        output_proj,
        output_bias,
        expand_weight,
        expand_bias,
        reduce_weight,
        reduce_bias,
    )
    stored_rows = stored.T
    cot_rows = cotangent.T
    forward_pass = forward(stored_rows, positions, segments, present, params)
    barrier_args = lax.optimization_barrier((stored_rows, params, forward_pass["output"]))
    kept_values = forward(barrier_args[0], positions, segments, present, barrier_args[1])
    model_size = lax.axis_size("mp")
    hidden_size = lax.axis_size("hidden")
    norm_rows = stored_rows.shape[0]
    split_rows = norm_rows * hidden_size // model_size
    feed_values = kept_values["feed_values"]
    out_rows = rows_hidden(cot_rows)
    d_reduce_bias = jnp.sum(out_rows, axis=0, dtype=jnp.float32)
    d_reduce = jnp.einsum(
        "rf,rd->df", feed_values["act_low"], out_rows, preferred_element_type=jnp.float32
    )
    act_grad = sum_model(row_product(out_rows, reduce_weight, 0), split_rows)
    pre_grad = (act_grad * gelu_slope(feed_values["pre_act"])).astype(jnp.bfloat16)
    pre_rows = rows_model(pre_grad)
    d_expand = jnp.einsum(
        "rd,rf->df", feed_values["tokens"], pre_rows, preferred_element_type=jnp.float32
    )
    d_expand_bias = jnp.sum(pre_rows, axis=0, dtype=jnp.float32)
    second_grad = sum_hidden(row_product(pre_rows, expand_weight, 1), norm_rows)
    middle_grad = cot_rows.astype(jnp.float32) + norm_back(
        second_grad, kept_values["second_normed"], kept_values["second_scale"], norm_gains[1]
    )
    gain_second = jnp.sum(second_grad * kept_values["second_normed"], axis=0)
    shift_second = jnp.sum(second_grad, axis=0)
    branch_low = middle_grad.astype(jnp.bfloat16)
    middle_rows = rows_hidden(branch_low)
    d_output_bias = jnp.sum(middle_rows, axis=0, dtype=jnp.float32)
    d_output = jnp.einsum(
        "rc,rd->cd", kept_values["att_rows"], middle_rows, preferred_element_type=jnp.float32
    )
    att_grad = sum_model(
        row_product(regroup(middle_rows, hidden_size, model_size), output_proj, 1), split_rows
    )
    att_heads = into_heads(att_grad.astype(jnp.bfloat16).reshape(split_rows, 1, -1))
    head_grad = attend_back(
        kept_values["head_layout"],
        att_heads.reshape(att_heads.shape[0], -1),
        kept_values["log_sums"],
        segments,
        present,
    )
    qkv_cols = from_heads(head_grad.astype(jnp.bfloat16))
    qkv_rows = rows_model(qkv_cols)
    d_input = jnp.einsum(
        "rd,rkc->dkc", kept_values["first_rows"], qkv_rows, preferred_element_type=jnp.float32
    )
    bias_sums = jnp.sum(qkv_rows, axis=0, dtype=jnp.float32)
    d_input_bias = jnp.stack([bias_sums[0], bias_sums[2]])
    flat_input = input_proj.reshape(input_proj.shape[0], -1)
    qkv_back = regroup(qkv_rows.reshape(qkv_rows.shape[0], -1), model_size, hidden_size)
    first_grad = sum_hidden(row_product(qkv_back, flat_input, 1), norm_rows)
    stored_grad = middle_grad + norm_back(
        first_grad, kept_values["first_normed"], kept_values["first_scale"], norm_gains[0]
    )
    gain_first = jnp.sum(first_grad * kept_values["first_normed"], axis=0)
    shift_first = jnp.sum(first_grad, axis=0)
    weight_parts = (
        lax.psum_scatter(
            d_input.astype(jnp.bfloat16), "dp", scatter_dimension=0, tiled=True
        ).astype(jnp.float32),
        lax.psum_scatter(
            d_input_bias.astype(jnp.bfloat16), "dp", scatter_dimension=1, tiled=True
        ).astype(jnp.float32),
        lax.psum_scatter(
            d_output.astype(jnp.bfloat16), "dp", scatter_dimension=0, tiled=True
        ).astype(jnp.float32),
        lax.psum_scatter(
            d_output_bias.astype(jnp.bfloat16), "dp", scatter_dimension=0, tiled=True
        ).astype(jnp.float32),
        lax.psum_scatter(
            d_expand.astype(jnp.bfloat16), "dp", scatter_dimension=0, tiled=True
        ).astype(jnp.float32),
        lax.psum_scatter(
            d_expand_bias.astype(jnp.bfloat16), "dp", scatter_dimension=0, tiled=True
        ).astype(jnp.float32),
        lax.psum_scatter(
            d_reduce.astype(jnp.bfloat16), "dp", scatter_dimension=0, tiled=True
        ).astype(jnp.float32),
        lax.psum_scatter(
            d_reduce_bias.astype(jnp.bfloat16), "dp", scatter_dimension=0, tiled=True
        ).astype(jnp.float32),
    )
    norm_parts = (
        lax.psum_scatter(
            jnp.stack([gain_first, gain_second]), ("dp", "hidden"), scatter_dimension=1, tiled=True
        ),
        lax.psum_scatter(
            jnp.stack([shift_first, shift_second]),
            ("dp", "hidden"),
            scatter_dimension=1,
            tiled=True,
        ),
    )
    return (
        forward_pass["output"].astype(jnp.bfloat16).T,
        stored_grad.T,
        norm_parts[0],
        norm_parts[1],
        weight_parts[0],
        weight_parts[1],
        weight_parts[2],
        weight_parts[3],
        weight_parts[4],
        weight_parts[5],
        weight_parts[6],
        weight_parts[7],
    )


def solution(mesh):
    placed = (
        P("mp", ("dp", "hidden")),
        P(("dp", "hidden")),
        P(("dp", "hidden", "mp")),
        P(("dp", "hidden", "mp")),
        P(None, "mp"),
        P(None, "mp"),
        P("mp", None, "hidden"),
        P(None, "hidden"),
        P("hidden", "mp"),
        P("mp"),
        P("mp", "hidden"),
        P("hidden"),
        P("mp", "hidden"),
        P("mp"),
        P("mp", ("dp", "hidden")),
    )
    return jax.shard_map(
        local,
        mesh=mesh,
        in_specs=placed,
        out_specs=(
            P("mp", ("dp", "hidden")),
            P("mp", ("dp", "hidden")),
            P(None, ("mp", "dp", "hidden")),
            P(None, ("mp", "dp", "hidden")),
            P(("mp", "dp"), None, "hidden"),
            P(None, ("hidden", "dp")),
            P(("hidden", "dp"), "mp"),
            P(("mp", "dp")),
            P(("mp", "dp"), "hidden"),
            P(("hidden", "dp")),
            P(("mp", "dp"), "hidden"),
            P(("mp", "dp")),
        ),
        check_vma=False,
    )
```

profile of v0, /device:TPU:0, one launch (start us, length us, event | category | flops | bytes accessed | tf_op | source)
XLA Modules:
  0.0 6484.3 jit_solution(10218393587834596029)
XLA Ops:
  24.4 17.8 all-reduce.11
  56.6 114.4 %all-gather.13.cloned.1.call-done = bf16[16384,192]{0,1:T(8,128)(2,1)} async-done(((bf16[4096,192]{0,1:T(8,128)(2,1)}), bf16[16384,192]{0,1:T(8,128)(2,1)}) %all-gather.13.cloned.1.call-update) | async-done | bytes 6291472 | tf_op jit(solution)/shard_map/all_gather | solution.py:59
  223.8 319.6 %reduce-scatter.21.cloned.1.call-done = f32[4096,576]{0,1:T(8,128)} async-done(((f32[16384,576]{0,1:T(8,128)}), f32[4096,576]{0,1:T(8,128)}) %reduce-scatter.21.cloned.1.call-update) | async-done | bytes 9437200 | tf_op jit(solution)/shard_map/reduce_scatter | solution.py:67
  569.5 183.3 %all-to-all-done = bf16[4096,3,192]{2,1,0:T(4,128)(2,1)} async-done(((bf16[4096,3,192]{2,1,0:T(4,128)(2,1)}), bf16[4096,3,192]{2,1,0:T(4,128)(2,1)}, u32[]{:S(2)}, u32[]{:S(2)}) %all-to-all-start) | async-done | bytes 4718624 | tf_op jit(solution)/shard_map/all_to_all | solution.py:85
  771.2 116.2 %while.62 = (s32[]{:T(128)}, bf16[2,512,12,64]{1,3,2,0:T(8,128)(2,1)}, s32[2]{0:T(128)S(1)}, s32[1024]{0:T(1024)S(1)}, s32[1024]{0:T(1024)S(1)}, /*index=5*/bf16...) while((s32[]{:T(128)}, ...), condition=%wide.region_8.9_spmd, body=%wide.region_5.8_spmd.sunk | while | flops 1663044096 | bytes 107287224 | solution.py:141
  784.0 33.6 fusion.163
  842.1 33.6 fusion.163
  915.3 39.7 all_to_all.93
  961.7 68.4 %all-gather.15.cloned.1.call-done = bf16[16384,192]{0,1:T(8,128)(2,1)} async-done(((bf16[4096,192]{0,1:T(8,128)(2,1)}), bf16[16384,192]{0,1:T(8,128)(2,1)}) %all-gather.15.cloned.1.call-update) | async-done | bytes 6291472 | tf_op jit(solution)/shard_map/all_gather | solution.py:63
  1074.4 211.4 %reduce-scatter.23.cloned.1.call-done = f32[4096,192]{0,1:T(8,128)} async-done(((f32[16384,192]{0,1:T(8,128)}), f32[4096,192]{0,1:T(8,128)}) %reduce-scatter.23.cloned.1.call-update) | async-done | bytes 3145744 | tf_op jit(solution)/shard_map/reduce_scatter | solution.py:76
  1320.6 114.7 %all-gather.17.cloned.1.call-done = bf16[16384,192]{0,1:T(8,128)(2,1)} async-done(((bf16[4096,192]{0,1:T(8,128)(2,1)}), bf16[16384,192]{0,1:T(8,128)(2,1)}) %all-gather.17.cloned.1.call-update) | async-done | bytes 6291472 | tf_op jit(solution)/shard_map/all_gather | solution.py:59
  1435.3 21.1 fusion.87
  1457.2 421.8 %reduce-scatter.25.cloned.1.call-done = f32[4096,768]{1,0:T(8,128)} async-done(((f32[16384,768]{1,0:T(8,128)}), f32[4096,768]{1,0:T(8,128)}) %reduce-scatter.25.cloned.1.call-update) | async-done | bytes 12582928 | tf_op jit(solution)/shard_map/reduce_scatter | solution.py:67
  1878.9 30.0 fusion.42
  1909.0 227.8 %all-gather.19.cloned.1.call-done = bf16[16384,768]{1,0:T(8,128)(2,1)} async-done(((bf16[4096,768]{1,0:T(8,128)(2,1)}), bf16[16384,768]{1,0:T(8,128)(2,1)}) %all-gather.19.cloned.1.call-update) | async-done | bytes 25165840 | tf_op jit(solution)/shard_map/all_gather | solution.py:63
  2153.1 211.4 %reduce-scatter.27.cloned.1.call-done = f32[4096,192]{0,1:T(8,128)} async-done(((f32[16384,192]{0,1:T(8,128)}), f32[4096,192]{0,1:T(8,128)}) %reduce-scatter.27.cloned.1.call-update) | async-done | bytes 3145744 | tf_op jit(solution)/shard_map/reduce_scatter | solution.py:76
  2411.6 114.5 %all-gather.21.cloned.1.call-done = bf16[16384,192]{0,1:T(8,128)(2,1)} async-done(((bf16[4096,192]{0,1:T(8,128)(2,1)}), bf16[16384,192]{0,1:T(8,128)(2,1)}) %all-gather.21.cloned.1.call-update) | async-done | bytes 6291472 | tf_op jit(solution)/shard_map/all_gather | solution.py:59
  2578.7 320.1 %reduce-scatter.29.cloned.1.call-done = f32[4096,576]{0,1:T(8,128)} async-done(((f32[16384,576]{0,1:T(8,128)}), f32[4096,576]{0,1:T(8,128)}) %reduce-scatter.29.cloned.1.call-update) | async-done | bytes 9437200 | tf_op jit(solution)/shard_map/reduce_scatter | solution.py:67
  2924.9 183.2 %all-to-all-done.2 = bf16[4096,3,192]{2,1,0:T(4,128)(2,1)} async-done(((bf16[4096,3,192]{2,1,0:T(4,128)(2,1)}), bf16[4096,3,192]{2,1,0:T(4,128)(2,1)}, u32[]{:S(2)}, u32[]{:S(2)}) %all-to-all-start.2) | async-done | bytes 4718624 | tf_op jit(solution)/shard_map/all_to_all | solution.py:85
  3126.4 73.1 %while.63 = (s32[]{:T(128)}, bf16[2,512,12,64]{1,3,2,0:T(8,128)(2,1)}, f32[2,12,512]{2,1,0:T(8,128)S(1)}, s32[2]{0:T(128)S(1)}, s32[1024]{0:T(1024)S(1)}, /*inde...) while((s32[]{:T(128)}, ...), condition=%wide.region_24.25_spmd, body=%wide.region_21.24_spmd.sunk | while | flops 1688202752 | bytes 190296816 | solution.py:141
  3232.1 40.9 all_to_all.94
  3279.7 68.4 %all-gather.23.cloned.1.call-done = bf16[16384,192]{0,1:T(8,128)(2,1)} async-done(((bf16[4096,192]{0,1:T(8,128)(2,1)}), bf16[16384,192]{0,1:T(8,128)(2,1)}) %all-gather.23.cloned.1.call-update) | async-done | bytes 6291472 | tf_op jit(solution)/shard_map/all_gather | solution.py:63
  3393.1 210.6 %reduce-scatter.31.cloned.1.call-done = f32[4096,192]{0,1:T(8,128)} async-done(((f32[16384,192]{0,1:T(8,128)}), f32[4096,192]{0,1:T(8,128)}) %reduce-scatter.31.cloned.1.call-update) | async-done | bytes 3145744 | tf_op jit(solution)/shard_map/reduce_scatter | solution.py:76
  3640.0 81.9 %all-gather.25.cloned.1.call-done = bf16[16384,192]{0,1:T(8,128)(2,1)} async-done(((bf16[4096,192]{0,1:T(8,128)(2,1)}), bf16[16384,192]{0,1:T(8,128)(2,1)}) %all-gather.25.cloned.1.call-update) | async-done | bytes 6291472 | tf_op jit(solution)/shard_map/all_gather | solution.py:59
  3721.8 23.0 fusion.90
  3744.9 92.6 %all-gather.27.cloned.1.call-done = bf16[16384,192]{0,1:T(8,128)(2,1)} async-done(((bf16[4096,192]{0,1:T(8,128)(2,1)}), bf16[16384,192]{0,1:T(8,128)(2,1)}) %all-gather.27.cloned.1.call-update) | async-done | bytes 6291472 | tf_op jit(solution)/shard_map/all_gather | solution.py:59
  3837.5 22.7 fusion.91
  3861.5 401.5 %reduce-scatter.33.cloned.1.call-done = f32[4096,768]{1,0:T(8,128)} async-done(((f32[16384,768]{1,0:T(8,128)}), f32[4096,768]{1,0:T(8,128)}) %reduce-scatter.33.cloned.1.call-update) | async-done | bytes 12582928 | tf_op jit(solution)/shard_map/reduce_scatter | solution.py:67
  4263.1 427.1 %reduce-scatter.35.cloned.1.call-done = f32[4096,768]{1,0:T(8,128)} async-done(((f32[16384,768]{1,0:T(8,128)}), f32[4096,768]{1,0:T(8,128)}) %reduce-scatter.35.cloned.1.call-update) | async-done | bytes 12582928 | tf_op jit(solution)/shard_map/reduce_scatter | solution.py:67
  4690.1 36.2 fusion.51
  4726.4 227.8 %all-gather.29.cloned.1.call-done = bf16[16384,768]{1,0:T(8,128)(2,1)} async-done(((bf16[4096,768]{1,0:T(8,128)(2,1)}), bf16[16384,768]{1,0:T(8,128)(2,1)}) %all-gather.29.cloned.1.call-update) | async-done | bytes 25165840 | tf_op jit(solution)/shard_map/all_gather | solution.py:63
  4969.9 212.0 %reduce-scatter.37.cloned.1.call-done = f32[4096,192]{0,1:T(8,128)} async-done(((f32[16384,192]{0,1:T(8,128)}), f32[4096,192]{0,1:T(8,128)}) %reduce-scatter.37.cloned.1.call-update) | async-done | bytes 3145744 | tf_op jit(solution)/shard_map/reduce_scatter | solution.py:76
  5211.2 114.3 %all-gather.31.cloned.1.call-done = bf16[16384,192]{0,1:T(8,128)(2,1)} async-done(((bf16[4096,192]{0,1:T(8,128)(2,1)}), bf16[16384,192]{0,1:T(8,128)(2,1)}) %all-gather.31.cloned.1.call-update) | async-done | bytes 6291472 | tf_op jit(solution)/shard_map/all_gather | solution.py:59
  5369.6 118.3 %reduce-scatter.39.cloned.1.call-done = f32[4096,192]{0,1:T(8,128)} async-done(((f32[16384,192]{0,1:T(8,128)}), f32[4096,192]{0,1:T(8,128)}) %reduce-scatter.39.cloned.1.call-update) | async-done | bytes 3145744 | tf_op jit(solution)/shard_map/reduce_scatter | solution.py:67
  5503.6 36.9 all-to-all-done.4
  5560.2 181.0 %while.64 = (s32[]{:T(128)}, f32[1024,12,64]{0,2,1:T(8,128)}, f32[1024,12,64]{0,2,1:T(8,128)}, bf16[2,512,12,64]{1,3,2,0:T(8,128)(2,1)}, s32[2]{0:T(128)S(1)}, /...) while((s32[]{:T(128)}, f32[1024,12,64]{0,2,1:T(8,128)}, ...), condition=%wide.region_40.41_spmd.clone, body=%wide.region_38.40_spmd.clone.sunk | while | flops 4127321600 | bytes 213054256 | solution.py:189
  5575.8 23.5 multiply_reduce_fusion.12
  5599.3 21.3 multiply_convert_fusion.2
  5667.7 18.2 multiply_reduce_fusion.12
  5685.9 21.3 multiply_convert_fusion.2
  5760.5 138.1 %all_to_all.95 = bf16[1024,3,768]{0,1,2:T(4,128)(2,1)S(1)} all-to-all(bf16[1024,3,768]{0,1,2:T(4,128)(2,1)S(1)} %copy.142), channel_id=1, replica_groups=mesh['dp'=2,'mp'=4,'hidden'=4] {'hidden'}, dimensions={2} | all-to-all | bytes 9437184 | tf_op jit(solution)/shard_map/all_to_all | solution.py:89
  5955.4 121.5 %all-gather.33.cloned.1.call-done = bf16[16384,3,192]{0,2,1:T(8,128)(2,1)} async-done(((bf16[4096,3,192]{0,2,1:T(8,128)(2,1)}), bf16[16384,3,192]{0,2,1:T(8,128)(2,1)}) %all-gather.33.cloned.1.call-update) | async-done | bytes 18874384 | tf_op jit(solution)/shard_map/all_gather | solution.py:63
  6099.8 31.2 reshape_reshape.4
  6131.1 18.4 copy.162
  6149.5 31.1 reshape.491
  6200.9 18.3 reduce_sum.234
  6239.6 164.8 %reduce-scatter.41.cloned.1.call-done = f32[4096,192]{0,1:T(8,128)} async-done(((f32[16384,192]{0,1:T(8,128)}), f32[4096,192]{0,1:T(8,128)}) %reduce-scatter.41.cloned.1.call-update) | async-done | bytes 3145744 | tf_op jit(solution)/shard_map/reduce_scatter | solution.py:76
  6441.9 17.7 all-reduce.6
  (393 shorter events, 1052.2 us)
Async XLA Ops:
  7.2 1428.1 %copy-start = (bf16[192,768]{1,0:T(8,128)(2,1)S(1)}, bf16[192,768]{1,0:T(8,128)(2,1)}, u32[]{:S(2)}) copy-start(bf16[192,768]{1,0:T(8,128)(2,1)} %param.31) | copy-start | bytes 884740
  7.2 163.8 %all-gather.13.cloned.1.call-start = ((), (), s32[]{:S(2)}) async-start(), calls=%async_computation.22 | async-start | bytes 7864320 | tf_op jit(solution)/shard_map/all_gather | solution.py:59
  56.1 487.3 %reduce-scatter.21.cloned.1.call-start = ((), (), s32[]{:S(2)}) async-start(), calls=%async_computation.23 | async-start | bytes 47185920 | tf_op jit(solution)/shard_map/reduce_scatter | solution.py:67
  563.4 189.4 %all-to-all-start = ((bf16[4096,3,192]{2,1,0:T(4,128)(2,1)}), bf16[4096,3,192]{2,1,0:T(4,128)(2,1)}, u32[]{:S(2)}, u32[]{:S(2)}) async-start(bf16[4096,3,192]{2,1,0:T(4,128)(2,1)} %copy.123), calls=%async_computation.1 | async-start | bytes 16777216 | tf_op jit(solution)/shard_map/all_to_all | solution.py:85
  569.5 460.6 %all-gather.15.cloned.1.call-start = ((), (), s32[]{:S(2)}) async-start(), calls=%async_computation.24 | async-start | bytes 7864320 | tf_op jit(solution)/shard_map/all_gather | solution.py:63
  961.7 324.1 %reduce-scatter.23.cloned.1.call-start = ((), (), s32[]{:S(2)}) async-start(), calls=%async_computation.25 | async-start | bytes 15728640 | tf_op jit(solution)/shard_map/reduce_scatter | solution.py:76
  1073.8 212.0 %copy-start.28 = (f32[4096]{0:T(1024)S(1)}, f32[4096]{0:T(1024)}, u32[]{:S(2)}) copy-start(f32[4096]{0:T(1024)} %copy-done.27) | copy-start | bytes 49156
  1073.8 212.0 %copy-start.46 = (f32[192]{0:T(256)S(1)}, f32[192]{0:T(256)}, u32[]{:S(2)}) copy-start(f32[192]{0:T(256)} %copy-done.45) | copy-start | bytes 2308
  1073.8 243.1 %copy-start.47 = (f32[1,192]{1,0:T(1,128)S(1)}, f32[1,192]{1,0:T(1,128)}, u32[]{:S(2)}) copy-start(f32[1,192]{1,0:T(1,128)} %get-tuple-element.404) | copy-start | bytes 2308
  1073.8 243.1 %copy-start.56 = (f32[1,192]{1,0:T(1,128)S(1)}, f32[1,192]{1,0:T(1,128)}, u32[]{:S(2)}) copy-start(f32[1,192]{1,0:T(1,128)} %get-tuple-element.406) | copy-start | bytes 2308
  1073.8 361.5 %all-gather.17.cloned.1.call-start = ((), (), s32[]{:S(2)}) async-start(), calls=%async_computation.26 | async-start | bytes 7864320 | tf_op jit(solution)/shard_map/all_gather | solution.py:59
  1320.6 558.4 %reduce-scatter.25.cloned.1.call-start = ((), (), s32[]{:S(2)}) async-start(), calls=%async_computation.27 | async-start | bytes 62914560 | tf_op jit(solution)/shard_map/reduce_scatter | solution.py:67
  1456.5 680.3 %all-gather.19.cloned.1.call-start = ((), (), s32[]{:S(2)}) async-start(), calls=%async_computation.28 | async-start | bytes 31457280 | tf_op jit(solution)/shard_map/all_gather | solution.py:63
  1909.0 227.9 %copy-start.22 = (bf16[192,768]{1,0:T(8,128)(2,1)S(1)}, bf16[192,768]{1,0:T(8,128)(2,1)}, u32[]{:S(2)}) copy-start(bf16[192,768]{1,0:T(8,128)(2,1)} %param.33) | copy-start | bytes 884740
  1909.0 455.5 %reduce-scatter.27.cloned.1.call-start = ((), (), s32[]{:S(2)}) async-start(), calls=%async_computation.29 | async-start | bytes 15728640 | tf_op jit(solution)/shard_map/reduce_scatter | solution.py:76
  2152.5 245.3 %copy-start.54 = (f32[2,192]{1,0:T(2,128)S(1)}, f32[2,192]{1,0:T(2,128)}, u32[]{:S(2)}) copy-start(f32[2,192]{1,0:T(2,128)} %param.26) | copy-start | bytes 4612
  2152.5 245.3 %copy-start.55 = (f32[2,192]{1,0:T(2,128)S(1)}, f32[2,192]{1,0:T(2,128)}, u32[]{:S(2)}) copy-start(f32[2,192]{1,0:T(2,128)} %param.25) | copy-start | bytes 4612
  2152.5 373.6 %all-gather.21.cloned.1.call-start = ((), (), s32[]{:S(2)}) async-start(), calls=%async_computation.30 | async-start | bytes 7864320 | tf_op jit(solution)/shard_map/all_gather | solution.py:59
  2153.1 258.3 %copy-start.21 = (bf16[192,3,192]{2,0,1:T(8,128)(2,1)S(1)}, bf16[192,3,192]{2,0,1:T(8,128)(2,1)}, u32[]{:S(2)}) copy-start(bf16[192,3,192]{2,0,1:T(8,128)(2,1)} %param.27) | copy-start | bytes 663556
  2411.3 487.5 %reduce-scatter.29.cloned.1.call-start = ((), (), s32[]{:S(2)}) async-start(), calls=%async_computation.31 | async-start | bytes 47185920 | tf_op jit(solution)/shard_map/reduce_scatter | solution.py:67
  2918.7 189.4 %all-to-all-start.2 = ((bf16[4096,3,192]{2,1,0:T(4,128)(2,1)}), bf16[4096,3,192]{2,1,0:T(4,128)(2,1)}, u32[]{:S(2)}, u32[]{:S(2)}) async-start(bf16[4096,3,192]{2,1,0:T(4,128)(2,1)} %copy.131), calls=%async_computation.7 | async-start | bytes 16777216 | tf_op jit(solution)/shard_map/all_to_all | solution.py:85
  2924.8 423.3 %all-gather.23.cloned.1.call-start = ((), (), s32[]{:S(2)}) async-start(), calls=%async_computation.32 | async-start | bytes 7864320 | tf_op jit(solution)/shard_map/all_gather | solution.py:63
  3279.7 324.1 %reduce-scatter.31.cloned.1.call-start = ((), (), s32[]{:S(2)}) async-start(), calls=%async_computation.33 | async-start | bytes 15728640 | tf_op jit(solution)/shard_map/reduce_scatter | solution.py:76
  3391.7 212.0 %copy-start.29 = (f32[4096]{0:T(1024)S(1)}, f32[4096]{0:T(1024)}, u32[]{:S(2)}) copy-start(f32[4096]{0:T(1024)} %copy-done.27) | copy-start | bytes 49156
  3391.7 330.1 %all-gather.25.cloned.1.call-start = ((), (), s32[]{:S(2)}) async-start(), calls=%async_computation.34 | async-start | bytes 7864320 | tf_op jit(solution)/shard_map/all_gather | solution.py:59
  3392.5 445.0 %all-gather.27.cloned.1.call-start = ((), (), s32[]{:S(2)}) async-start(), calls=%async_computation.36 | async-start | bytes 7864320 | tf_op jit(solution)/shard_map/all_gather | solution.py:59
  3618.5 1587.0 %copy-start.6 = (f32[4096,192]{0,1:T(8,128)}, f32[4096,192]{0,1:T(8,128)S(1)}, u32[]{:S(2)}) copy-start(f32[4096,192]{0,1:T(8,128)S(1)} %get-tuple-element.374) | copy-start | bytes 9437188
  3636.9 1568.6 %copy-start.33 = (f32[4096]{0:T(1024)}, f32[4096]{0:T(1024)S(1)}, u32[]{:S(2)}) copy-start(f32[4096]{0:T(1024)S(1)} %get-tuple-element.390) | copy-start | bytes 49156
  3639.9 623.1 %reduce-scatter.33.cloned.1.call-start = ((), (), s32[]{:S(2)}) async-start(), calls=%async_computation.35 | async-start | bytes 62914560 | tf_op jit(solution)/shard_map/reduce_scatter | solution.py:67
  3744.8 945.3 %reduce-scatter.35.cloned.1.call-start = ((), (), s32[]{:S(2)}) async-start(), calls=%async_computation.37 | async-start | bytes 62914560 | tf_op jit(solution)/shard_map/reduce_scatter | solution.py:67
  3860.2 1094.0 %all-gather.29.cloned.1.call-start = ((), (), s32[]{:S(2)}) async-start(), calls=%async_computation.38 | async-start | bytes 31457280 | tf_op jit(solution)/shard_map/all_gather | solution.py:63
  4726.4 455.5 %reduce-scatter.37.cloned.1.call-start = ((), (), s32[]{:S(2)}) async-start(), calls=%async_computation.39 | async-start | bytes 15728640 | tf_op jit(solution)/shard_map/reduce_scatter | solution.py:76
  4969.9 355.6 %all-gather.31.cloned.1.call-start = ((), (), s32[]{:S(2)}) async-start(), calls=%async_computation.40 | async-start | bytes 7864320 | tf_op jit(solution)/shard_map/all_gather | solution.py:59
  5210.7 277.2 %reduce-scatter.39.cloned.1.call-start = ((), (), s32[]{:S(2)}) async-start(), calls=%async_computation.41 | async-start | bytes 15728640 | tf_op jit(solution)/shard_map/reduce_scatter | solution.py:67
  5368.9 563.5 %all-gather.35.cloned.1.call-start = ((), (), s32[]{:S(2)}) async-start(), calls=%async_computation.47 | async-start | bytes 31457280 | tf_op jit(solution)/shard_map/all_gather | solution.py:63
  5499.0 41.6 all-to-all-start.4
  5503.6 573.3 %all-gather.33.cloned.1.call-start = ((), (), s32[]{:S(2)}) async-start(), calls=%async_computation.42 | async-start | bytes 23592960 | tf_op jit(solution)/shard_map/all_gather | solution.py:63
  5903.5 315.8 %reduce-scatter.47.cloned.1.call-start = ((), (), s32[]{:S(2)}) async-start(), calls=%async_computation.46 | async-start | bytes 442368 | tf_op jit(solution)/shard_map/reduce_scatter | solution.py:372
  5932.3 288.8 %reduce-scatter.49.cloned.1.call-start = ((), (), s32[]{:S(2)}) async-start(), calls=%async_computation.48 | async-start | bytes 442368 | tf_op jit(solution)/shard_map/reduce_scatter | solution.py:378
  5948.2 285.7 %reduce-scatter.45.cloned.1.call-start = ((), (), s32[]{:S(2)}) async-start(), calls=%async_computation.45 | async-start | bytes 147456 | tf_op jit(solution)/shard_map/reduce_scatter | solution.py:366
  5955.4 280.0 %reduce-scatter.51.cloned.1.call-start = ((), (), s32[]{:S(2)}) async-start(), calls=%async_computation.49 | async-start | bytes 73728
  6088.0 149.9 %reduce-scatter.43.cloned.1.call-start = ((), (), s32[]{:S(2)}) async-start(), calls=%async_computation.44 | async-start | bytes 442368 | tf_op jit(solution)/shard_map/reduce_scatter | solution.py:360
  6180.6 223.8 %reduce-scatter.41.cloned.1.call-start = ((), (), s32[]{:S(2)}) async-start(), calls=%async_computation.43 | async-start | bytes 15728640 | tf_op jit(solution)/shard_map/reduce_scatter | solution.py:76
  6219.2 241.8 %copy-start.7 = (f32[4096,192]{0,1:T(8,128)S(1)}, f32[4096,192]{0,1:T(8,128)}, u32[]{:S(2)}) copy-start(f32[4096,192]{0,1:T(8,128)} %copy-done.6) | copy-start | bytes 9437188
  6219.2 241.8 %copy-start.34 = (f32[4096]{0:T(1024)S(1)}, f32[4096]{0:T(1024)}, u32[]{:S(2)}) copy-start(f32[4096]{0:T(1024)} %copy-done.33) | copy-start | bytes 49156
  6219.2 241.8 %copy-start.36 = (f32[4096]{0:T(1024)S(1)}, f32[4096]{0:T(1024)}, u32[]{:S(2)}) copy-start(f32[4096]{0:T(1024)} %copy-done.35) | copy-start | bytes 49156
  6219.2 241.8 %copy-start.42 = (f32[4096]{0:T(1024)S(1)}, f32[4096]{0:T(1024)}, u32[]{:S(2)}) copy-start(f32[4096]{0:T(1024)} %copy-done.41) | copy-start | bytes 49156
  6219.2 241.8 %copy-start.44 = (f32[4096]{0:T(1024)S(1)}, f32[4096]{0:T(1024)}, u32[]{:S(2)}) copy-start(f32[4096]{0:T(1024)} %copy-done.43) | copy-start | bytes 49156
  (49 other events, 1751.1 us)
Sparse Core Ops, SparseCore 0:
  56.2 114.7 all-gather.12
  222.7 320.6 reduce-scatter.20
  961.8 68.2 all-gather.14
  1073.9 211.8 reduce-scatter.22
  1320.7 114.6 all-gather.16
  1456.6 422.2 reduce-scatter.24
  1909.1 227.6 all-gather.18
  2152.6 211.8 reduce-scatter.26
  2411.4 114.6 all-gather.20
  2578.0 320.6 reduce-scatter.28
  3279.8 68.2 all-gather.22
  3391.9 211.8 reduce-scatter.30
  3605.4 116.3 all-gather.24
  3723.9 113.5 all-gather.26
  3840.7 422.2 reduce-scatter.32
  4266.0 424.0 reduce-scatter.34
  4726.5 227.6 all-gather.28
  4970.0 211.8 reduce-scatter.36
  5210.8 114.6 all-gather.30
  5369.0 118.8 reduce-scatter.38
  5489.9 227.7 all-gather.34
  5903.6 173.2 all-gather.32
  6079.9 7.6 reduce-scatter.46
  6090.3 8.8 reduce-scatter.48
  6102.1 8.6 reduce-scatter.44
  6112.8 8.5 reduce-scatter.50
  6180.7 7.7 reduce-scatter.42
  6192.5 211.8 reduce-scatter.40
where the time goes:
time: 6500 us; the launch traced here: 6480 us
  waiting for transfers between devices  4770 us (73%)
  local copies, waits for them, and re-layouts  449 us (7%)
  other arithmetic  443 us (7%)
  matrix products  436 us (7%)
  blocking collectives  342 us (5%)
    reduce_scatter x6, waiting for transfers between devices, sum_model(): lax.psum_scatter(partial_term(jnp.int32(0), row_total * lax.axis_size('mp...  2010 us
    reduce_scatter x5, waiting for transfers between devices, sum_hidden(): lax.psum_scatter(partial_term(jnp.int32(0), row_total * lax.axis_size('hi...  1010 us
    all_gather x6, waiting for transfers between devices, rows_model(): return lax.all_gather(values, 'mp', axis=0, tiled=True)  714 us
    all_gather x6, waiting for transfers between devices, rows_hidden(): return lax.all_gather(values, 'hidden', axis=0, tiled=True)  632 us
    all_to_all x3, waiting for transfers between devices, into_heads(): lax.all_to_all(values, 'hidden', split_axis=0, concat_axis=2, tiled=True)  403 us
    all_to_all x3, blocking collectives, from_heads(): lax.all_to_all(values, 'hidden', split_axis=2, concat_axis=0, tiled=True)  219 us
    dot_general x11, matrix products, partial_term(): lax.dot_general(source, weight, (((1,), (contract,)), ((), ())), preferre...  172 us
  transfers between devices with their start and end apart: 31, of which 25 were waited for; matrix products, arithmetic and copies ran while one was open for 8% of the time, Pallas kernels for 0%

commit v1 on v0

v1 whole, which is shorter than its diff:
```python
import functools
import math

import jax
import jax.numpy as jnp
from jax import lax
from jax.experimental import pallas as pl
from jax.experimental.pallas import tpu as pltpu
from jax.sharding import PartitionSpec as P

D = 768
HEADS = 12
HD = 64
SEQ = 1024
FB = 256
QB = 256
PAIR = 2 * HD
PAIRS = HEADS // 2
EPS = 1e-06
MASKED = -1e30
F32 = jnp.float32
BF16 = jnp.bfloat16
VMEM_LIMIT = 60 * 1024 * 1024

NN = (((1,), (0,)), ((), ()))
NT = (((1,), (1,)), ((), ()))


def mm(a, b, dims=NN):
    return lax.dot_general(a, b, dims, preferred_element_type=F32)


def whole(shape):
    return pl.BlockSpec(shape, lambda *_: (0,) * len(shape), pipeline_mode=pl.Buffered(1))


def params(**kw):
    return pltpu.CompilerParams(vmem_limit_bytes=VMEM_LIMIT, **kw)


def lane_sums(x):
    total = x[:, 0:128]
    for j in range(1, x.shape[1] // 128):
        total = total + x[:, j * 128 : (j + 1) * 128]
    return total


def norm_stats(e):
    average = jnp.sum(e, axis=0, keepdims=True) * (1.0 / D)
    spread = jnp.sum(e * e, axis=0, keepdims=True) * (1.0 / D) - average * average
    return average, lax.rsqrt(spread + EPS)


def project_kernel(x_ref, tab_ref, g_ref, b_ref, w_ref, wb_ref, et_ref, ft_ref, qkv_ref, f_ref):
    def norm_cols(j, _):
        cols = pl.ds(pl.multiple_of(j * 256, 256), 256)
        e = x_ref[:, cols].astype(F32) + tab_ref[:, cols]
        et_ref[:, cols] = e
        average, inv = norm_stats(e)
        f = ((e - average) * inv * g_ref[...] + b_ref[...]).astype(BF16)
        ft_ref[:, cols] = f
        f_ref[cols, :] = f.T
        return 0

    lax.fori_loop(0, SEQ // 256, norm_cols, 0)

    def cols_of(n, scale):
        cols = pl.ds(pl.multiple_of(n * 256, 256), 256)
        y = (mm(f_ref[...], w_ref[:, cols]) + wb_ref[:, cols]).astype(BF16)
        qkv_ref[:, cols] = y * jnp.asarray(scale, BF16)
        return 0

    lax.fori_loop(0, D // 256, lambda n, c: cols_of(n, HD**-0.5), 0)
    lax.fori_loop(D // 256, 3 * D // 256, lambda n, c: cols_of(n, 1.0), 0)


def project(xt, table, gain, shift, w1, bias_row):
    return pl.pallas_call(
        project_kernel,
        out_shape=(
            jax.ShapeDtypeStruct((D, SEQ), F32),
            jax.ShapeDtypeStruct((D, SEQ), BF16),
            jax.ShapeDtypeStruct((SEQ, 3 * D), BF16),
        ),
        scratch_shapes=[pltpu.VMEM((SEQ, D), BF16)],
        compiler_params=params(),
        name="project",
    )(xt, table, gain, shift, w1, bias_row)


def fill_bias(bias_ref, key_ref, seg_ref):
    def rows_of(i, _):
        rows = pl.ds(pl.multiple_of(i * 256, 256), 256)
        same = key_ref[rows, :] == seg_ref[...]
        row_id = lax.broadcasted_iota(jnp.int32, (256, SEQ), 0) + i * 256
        col_id = lax.broadcasted_iota(jnp.int32, (256, SEQ), 1)
        bias_ref[rows, :] = jnp.where(same | (row_id == col_id), 0.0, MASKED)
        return 0

    lax.fori_loop(0, SEQ // 256, rows_of, 0)


def attend_kernel(q_ref, k_ref, v_ref, key_ref, seg_ref, at_ref, lse_ref, bias_ref, vt_ref):
    @pl.when(pl.program_id(0) == 0)
    def _():
        fill_bias(bias_ref, key_ref, seg_ref)

    vt_ref[...] = v_ref[...].T
    low = lax.broadcasted_iota(jnp.int32, (QB, PAIR), 1) < HD
    lse_ref[...] = jnp.zeros_like(lse_ref)

    def block(j, _):
        cols = pl.ds(pl.multiple_of(j * QB, QB), QB)
        q = q_ref[cols, :]
        for hh in range(2):
            qm = jnp.where(low if hh == 0 else ~low, q, jnp.zeros_like(q))
            s = mm(k_ref[...], qm, NT) + bias_ref[:, cols]
            top = jnp.max(s, axis=0, keepdims=True)
            p = jnp.exp(s - top)
            total = jnp.sum(p, axis=0, keepdims=True)
            o = mm(vt_ref[hh * HD : (hh + 1) * HD, :], p.astype(BF16)) / total
            at_ref[hh * HD : (hh + 1) * HD, cols] = o.astype(BF16)
            lse_ref[0, hh : hh + 1, cols] = top + jnp.log(total)
        return 0

    lax.fori_loop(0, SEQ // QB, block, 0)


def attend(qkv, key_col, seg_row):
    part = lambda k: pl.BlockSpec((SEQ, PAIR), lambda p: (0, k * PAIRS + p))
    return pl.pallas_call(
        attend_kernel,
        grid=(PAIRS,),
        in_specs=[part(0), part(1), part(2), whole((SEQ, 1)), whole((1, SEQ))],
        out_specs=(
            pl.BlockSpec((PAIR, SEQ), lambda p: (p, 0)),
            pl.BlockSpec((1, 8, SEQ), lambda p: (p, 0, 0)),
        ),
        out_shape=(
            jax.ShapeDtypeStruct((D, SEQ), BF16),
            jax.ShapeDtypeStruct((PAIRS, 8, SEQ), F32),
        ),
        scratch_shapes=[pltpu.VMEM((SEQ, SEQ), F32), pltpu.VMEM((PAIR, SEQ), BF16)],
        compiler_params=params(),
        name="attend",
    )(qkv, qkv, qkv, key_col, seg_row)


def feed_kernel(
    at_ref, et_ref, ct_ref, w2_ref, b2_ref, g_ref, b_ref, we_ref, be_ref, wr_ref, br_ref,
    out_ref, dmid_ref, do_ref, dwr_ref, dwe_ref, dbe_ref, dw2_ref, db_ref, dg_ref,
    s_ref, st_ref, c_ref, ot_ref, ds_ref, mid_ref, bt_ref,
):
    step = pl.program_id(0)

    @pl.when(step == 0)
    def _():
        w2t = w2_ref[...].T

        def cols_of(j, _):
            cols = pl.ds(pl.multiple_of(j * 256, 256), 256)
            mid = et_ref[:, cols] + (mm(w2t, at_ref[:, cols]) + b2_ref[...])
            mid_ref[:, cols] = mid
            average, inv = norm_stats(mid)
            s = ((mid - average) * inv * g_ref[...] + b_ref[...]).astype(BF16)
            st_ref[:, cols] = s
            s_ref[cols, :] = s.T
            c_ref[cols, :] = ct_ref[:, cols].T
            return 0

        lax.fori_loop(0, SEQ // 256, cols_of, 0)

    pre = mm(s_ref[...], we_ref[...]) + be_ref[...]
    cdf = 0.5 * (1.0 + lax.erf(pre * (1.0 / math.sqrt(2.0))))
    act = (pre * cdf).astype(BF16)
    slope = cdf + pre * jnp.exp(-0.5 * pre * pre) * (1.0 / math.sqrt(2.0 * math.pi))
    grad = (mm(c_ref[...], wr_ref[...]) * slope).astype(BF16)
    dwr_ref[...] = mm(ct_ref[...], act).astype(BF16)
    dwe_ref[...] = mm(st_ref[...], grad).astype(BF16)
    dbe_ref[...] = jnp.sum(grad.astype(F32), axis=0, keepdims=True)
    o = mm(wr_ref[...], act, NT)
    ds = mm(we_ref[...], grad, NT)

    @pl.when(step == 0)
    def _():
        ot_ref[...] = o
        ds_ref[...] = ds

    @pl.when(step > 0)
    def _():
        ot_ref[...] += o
        ds_ref[...] += ds

    @pl.when(step == pl.num_programs(0) - 1)
    def _():
        dg_ref[...] = jnp.zeros_like(dg_ref)

        def cols_of(j, _):
            cols = pl.ds(pl.multiple_of(j * 256, 256), 256)
            mid = mid_ref[:, cols]
            out_ref[:, cols] = (mid + (ot_ref[:, cols] + br_ref[...])).astype(BF16)
            average, inv = norm_stats(mid)
            normed = (mid - average) * inv
            ds = ds_ref[:, cols]
            scaled = ds * g_ref[...]
            total = jnp.sum(scaled, axis=0, keepdims=True) * (1.0 / D)
            crossed = jnp.sum(scaled * normed, axis=0, keepdims=True) * (1.0 / D)
            dmid = ct_ref[:, cols].astype(F32) + inv * (scaled - total - normed * crossed)
            dmid_ref[:, cols] = dmid
            low = dmid.astype(BF16)
            bt_ref[:, cols] = low
            do_ref[cols, :] = mm(w2_ref[...], low).astype(BF16).T
            dg_ref[0] += lane_sums(ds * normed)
            dg_ref[1] += lane_sums(ds)
            return 0

        lax.fori_loop(0, SEQ // 256, cols_of, 0)
        ones = jnp.ones((8, SEQ), BF16)
        db_ref[0] = mm(ones, ct_ref[...], NT)
        db_ref[1] = mm(ones, bt_ref[...], NT)

        def rows_of(j, _):
            rows = pl.ds(pl.multiple_of(j * 256, 256), 256)
            dw2_ref[rows, :] = mm(at_ref[rows, :], bt_ref[...], NT).astype(BF16)
            return 0

        lax.fori_loop(0, D // 256, rows_of, 0)


def feed(at, et, ct, w2, b2, gain, shift, we, be, wr, br):
    ff = we.shape[1]
    cols = pl.BlockSpec((D, FB), lambda f: (0, f))
    row = pl.BlockSpec((1, FB), lambda f: (0, f))
    sds = jax.ShapeDtypeStruct
    return pl.pallas_call(
        feed_kernel,
        grid=(ff // FB,),
        in_specs=[
            whole((D, SEQ)), whole((D, SEQ)), whole((D, SEQ)), whole((D, D)), whole((D, 1)), whole((D, 1)),
            whole((D, 1)), cols, row, cols, whole((D, 1)),
        ],
        out_specs=(
            whole((D, SEQ)), whole((D, SEQ)), whole((SEQ, D)), cols, cols, row, whole((D, D)),
            whole((2, 8, D)), whole((2, D, 128)),
        ),
        out_shape=(
            sds((D, SEQ), BF16), sds((D, SEQ), F32), sds((SEQ, D), BF16), sds((D, ff), BF16), sds((D, ff), BF16),
            sds((1, ff), F32), sds((D, D), BF16), sds((2, 8, D), F32), sds((2, D, 128), F32),
        ),
        scratch_shapes=[
            pltpu.VMEM((SEQ, D), BF16), pltpu.VMEM((D, SEQ), BF16), pltpu.VMEM((SEQ, D), BF16),
            pltpu.VMEM((D, SEQ), F32), pltpu.VMEM((D, SEQ), F32), pltpu.VMEM((D, SEQ), F32),
            pltpu.VMEM((D, SEQ), BF16),
        ],
        compiler_params=params(),
        name="feed",
    )(at, et, ct, w2, b2, gain, shift, we, be, wr, br)


def attend_back_kernel(
    q_ref, k_ref, v_ref, do_ref, lse_ref, key_ref, seg_ref, dqt_ref, dk_ref, dv_ref, bias_ref, kt_ref, dka_ref, dva_ref
):
    @pl.when(pl.program_id(0) == 0)
    def _():
        fill_bias(bias_ref, key_ref, seg_ref)

    kt_ref[...] = k_ref[...].T
    low = lax.broadcasted_iota(jnp.int32, (QB, PAIR), 1) < HD
    dka_ref[...] = jnp.zeros_like(dka_ref)
    dva_ref[...] = jnp.zeros_like(dva_ref)

    def block(j, _):
        cols = pl.ds(pl.multiple_of(j * QB, QB), QB)
        q = q_ref[cols, :]
        do = do_ref[cols, :]
        for hh in range(2):
            keep = low if hh == 0 else ~low
            qm = jnp.where(keep, q, jnp.zeros_like(q))
            dom = jnp.where(keep, do, jnp.zeros_like(do))
            p = jnp.exp(mm(k_ref[...], qm, NT) + bias_ref[:, cols] - lse_ref[0, hh : hh + 1, cols])
            t = p * mm(v_ref[...], dom, NT)
            ds = (t - p * jnp.sum(t, axis=0, keepdims=True)).astype(BF16)
            dva_ref[...] += mm(p.astype(BF16), dom)
            dka_ref[...] += mm(ds, qm)
            dq = mm(kt_ref[hh * HD : (hh + 1) * HD, :], ds) * HD**-0.5
            dqt_ref[hh * HD : (hh + 1) * HD, cols] = dq.astype(BF16)
        return 0

    lax.fori_loop(0, SEQ // QB, block, 0)
    dk_ref[...] = dka_ref[...].astype(BF16)
    dv_ref[...] = dva_ref[...].astype(BF16)


def attend_back(qkv, do, lse, key_col, seg_row):
    part = lambda k: pl.BlockSpec((SEQ, PAIR), lambda p: (0, k * PAIRS + p))
    return pl.pallas_call(
        attend_back_kernel,
        grid=(PAIRS,),
        in_specs=[
            part(0), part(1), part(2), part(0), pl.BlockSpec((1, 8, SEQ), lambda p: (p, 0, 0)),
            whole((SEQ, 1)), whole((1, SEQ)),
        ],
        out_specs=(pl.BlockSpec((PAIR, SEQ), lambda p: (p, 0)), part(0), part(0)),
        out_shape=(
            jax.ShapeDtypeStruct((D, SEQ), BF16),
            jax.ShapeDtypeStruct((SEQ, D), BF16),
            jax.ShapeDtypeStruct((SEQ, D), BF16),
        ),
        scratch_shapes=[
            pltpu.VMEM((SEQ, SEQ), F32), pltpu.VMEM((PAIR, SEQ), BF16),
            pltpu.VMEM((SEQ, PAIR), F32), pltpu.VMEM((SEQ, PAIR), F32),
        ],
        compiler_params=params(),
        name="attend_back",
    )(qkv, qkv, qkv, do, lse, key_col, seg_row)


def project_back_kernel(
    ft_ref, dqt_ref, dk_ref, dv_ref, w_ref, et_ref, dmid_ref, g_ref,
    dw_ref, dx_ref, db_ref, dg_ref, df_ref,
):
    df_ref[...] = jnp.zeros_like(df_ref)

    def cols_of(n, _):
        off = pl.multiple_of(n * 256, 256)
        cols = pl.ds(off, 256)
        dq = dqt_ref[cols, :]
        dk = dk_ref[:, cols]
        dv = dv_ref[:, cols]
        dw_ref[:, cols] = mm(ft_ref[...], dq, NT).astype(BF16)
        dw_ref[:, pl.ds(pl.multiple_of(off + D, 256), 256)] = mm(ft_ref[...], dk).astype(BF16)
        dw_ref[:, pl.ds(pl.multiple_of(off + 2 * D, 256), 256)] = mm(ft_ref[...], dv).astype(BF16)
        df_ref[...] += mm(w_ref[:, cols], dq)
        df_ref[...] += mm(w_ref[:, pl.ds(pl.multiple_of(off + D, 256), 256)], dk, NT)
        df_ref[...] += mm(w_ref[:, pl.ds(pl.multiple_of(off + 2 * D, 256), 256)], dv, NT)
        return 0

    lax.fori_loop(0, D // 256, cols_of, 0)
    ones = jnp.ones((8, SEQ), BF16)
    db_ref[0] = mm(ones, dqt_ref[...], NT)
    db_ref[1] = mm(ones, dv_ref[...])
    dg_ref[...] = jnp.zeros_like(dg_ref)

    def norm_cols(j, _):
        cols = pl.ds(pl.multiple_of(j * 256, 256), 256)
        e = et_ref[:, cols]
        average, inv = norm_stats(e)
        normed = (e - average) * inv
        df = df_ref[:, cols]
        scaled = df * g_ref[...]
        total = jnp.sum(scaled, axis=0, keepdims=True) * (1.0 / D)
        crossed = jnp.sum(scaled * normed, axis=0, keepdims=True) * (1.0 / D)
        dx_ref[:, cols] = (dmid_ref[:, cols] + inv * (scaled - total - normed * crossed)).astype(BF16)
        dg_ref[0] += lane_sums(df * normed)
        dg_ref[1] += lane_sums(df)
        return 0

    lax.fori_loop(0, SEQ // 256, norm_cols, 0)


def project_back(ft, dqt, dk, dv, w1, et, dmid, gain):
    sds = jax.ShapeDtypeStruct
    return pl.pallas_call(
        project_back_kernel,
        out_shape=(sds((D, 3 * D), BF16), sds((D, SEQ), BF16), sds((2, 8, D), F32), sds((2, D, 128), F32)),
        scratch_shapes=[pltpu.VMEM((D, SEQ), F32)],
        compiler_params=params(),
        name="project_back",
    )(ft, dqt, dk, dv, w1, et, dmid, gain)


def position_table(positions):
    rows = jnp.arange(D, dtype=jnp.int32)
    half = D // 2
    rates = jnp.exp((rows % half).astype(F32) * (-math.log(10000.0) / half))
    angles = rates[:, None] * positions.astype(F32)[None, :]
    return jnp.where(rows[:, None] < half, jnp.sin(angles), jnp.cos(angles))


GATHER = ("hidden", "mp", "dp")


def local(
    stored, positions, segments, present, norm_gains, norm_biases, input_proj, input_bias, output_proj,
    output_bias, expand_weight, expand_bias, reduce_weight, reduce_bias, cotangent,
):
    mp, hid, dp = lax.axis_size("mp"), lax.axis_size("hidden"), lax.axis_size("dp")
    m = lax.axis_index("mp")
    d = lax.axis_index("dp")
    rows_mp = D // mp
    half = rows_mp // dp
    cut = lambda w: lax.dynamic_slice_in_dim(w, d * half, half, 0)
    hcols = D // hid
    w1 = cut(input_proj).reshape(-1)
    we = cut(expand_weight).reshape(-1)
    wr = cut(reduce_weight).reshape(-1)
    w2 = lax.dynamic_slice_in_dim(output_proj, d * (hcols // dp), hcols // dp, 0).reshape(-1)
    sizes = [w1.size, w2.size, we.size, wr.size]
    flat = jnp.concatenate([w1, w2, we, wr]).reshape(-1, D)
    full = lax.all_gather(flat, GATHER, axis=0, tiled=True).reshape(hid, mp, dp, -1)
    o0, o1, o2 = sizes[0], sizes[0] + sizes[1], sizes[0] + sizes[1] + sizes[2]
    w1f = full[..., :o0].reshape(hid, D, 3, hcols).transpose(1, 2, 0, 3).reshape(D, 3 * D)
    w2f = full[..., o0:o1].reshape(hid, mp, dp, hcols // dp, rows_mp).transpose(0, 2, 3, 1, 4).reshape(D, D)
    fcols = expand_weight.shape[1]
    wef = full[..., o1:o2].reshape(hid, D, fcols).transpose(1, 0, 2).reshape(D, -1)
    wrf = full[..., o2:].reshape(hid, D, fcols).transpose(1, 0, 2).reshape(D, -1)
    gains, shifts = (lax.all_gather(t, "mp", axis=1, tiled=True) for t in (norm_gains, norm_biases))
    b2, br = (lax.all_gather(t, "mp", axis=0, tiled=True).astype(F32)[:, None] for t in (output_bias, reduce_bias))
    b1 = lax.all_gather(input_bias, "hidden", axis=1, tiled=True).astype(F32)
    be = lax.all_gather(expand_bias, "hidden", axis=0, tiled=True).astype(F32)[None]
    bias_row = jnp.concatenate([b1[0], jnp.zeros_like(b1[0]), b1[1]])[None]
    xt = lax.all_to_all(stored, "mp", split_axis=1, concat_axis=0, tiled=True)
    ct = lax.all_to_all(cotangent, "mp", split_axis=1, concat_axis=0, tiled=True)
    table = position_table(lax.dynamic_slice_in_dim(positions, m * SEQ, SEQ))
    key_col = jnp.where(present == 1, segments, -1)[:, None]
    seg_row = segments[None, :]

    et, ft, qkv = project(xt, table, gains[0][:, None], shifts[0][:, None], w1f, bias_row)
    at, lse = attend(qkv, key_col, seg_row)
    out_t, dmid, do, dwr, dwe, dbe, dw2, db_feed, dg_second = feed(
        at, et, ct, w2f, b2, gains[1][:, None], shifts[1][:, None], wef, be, wrf, br
    )
    dqt, dk, dv = attend_back(qkv, do, lse, key_col, seg_row)
    dw1, dx, db_proj, dg_first = project_back(ft, dqt, dk, dv, w1f, et, dmid, gains[0][:, None])

    output = lax.all_to_all(out_t, "mp", split_axis=0, concat_axis=1, tiled=True)
    d_stored = lax.all_to_all(dx, "mp", split_axis=0, concat_axis=1, tiled=True).astype(F32)

    n_parts = hid * mp * dp
    p1 = dw1.reshape(D, 3, hid, hcols).transpose(2, 0, 1, 3).reshape(n_parts, -1)
    p2 = dw2.reshape(hid, dp, hcols // dp, mp, rows_mp).transpose(0, 3, 1, 2, 4).reshape(n_parts, -1)
    pe = dwe.reshape(D, hid, fcols).transpose(1, 0, 2).reshape(n_parts, -1)
    pr = dwr.reshape(D, hid, fcols).transpose(1, 0, 2).reshape(n_parts, -1)
    packed = jnp.concatenate([p1, p2, pe, pr], axis=1).reshape(-1, D)
    mine = lax.psum_scatter(packed, GATHER, scatter_dimension=0, tiled=True).reshape(-1).astype(F32)
    d_input = mine[:o0].reshape(half, 3, hcols)
    d_output = mine[o0:o1].reshape(hcols // dp, rows_mp)
    d_expand = mine[o1:o2].reshape(half, fcols)
    d_reduce = mine[o2:].reshape(half, fcols)
    dg = jnp.stack([jnp.sum(dg_first, axis=2), jnp.sum(dg_second, axis=2)])
    vectors = jnp.concatenate(
        [dg.reshape(-1), db_proj[:, 0].reshape(-1), db_feed[:, 0].reshape(-1), dbe.reshape(-1)]
    )
    vectors = lax.psum(vectors, ("dp", "mp", "hidden"))
    h = lax.axis_index("hidden")
    dg = vectors[: 4 * D].reshape(2, 2, D)
    piece = D // n_parts
    dg = lax.dynamic_slice_in_dim(dg, ((m * dp + d) * hid + h) * piece, piece, 2)
    db_proj = vectors[4 * D : 6 * D].reshape(2, D)
    db_proj = lax.dynamic_slice_in_dim(db_proj, (h * dp + d) * (hcols // dp), hcols // dp, 1)
    db_feed = lax.dynamic_slice_in_dim(vectors[6 * D : 8 * D].reshape(2, D), (m * dp + d) * half, half, 1)
    dbe = lax.dynamic_slice_in_dim(vectors[8 * D :], (h * dp + d) * (fcols // dp), fcols // dp)
    return (
        output, d_stored, dg[:, 0], dg[:, 1], d_input, db_proj, d_output, db_feed[1], d_expand, dbe, d_reduce,
        db_feed[0],
    )


def solution(mesh):
    placed = (
        P("mp", ("dp", "hidden")),
        P(("dp", "hidden")),
        P(("dp", "hidden", "mp")),
        P(("dp", "hidden", "mp")),
        P(None, "mp"),
        P(None, "mp"),
        P("mp", None, "hidden"),
        P(None, "hidden"),
        P("hidden", "mp"),
        P("mp"),
        P("mp", "hidden"),
        P("hidden"),
        P("mp", "hidden"),
        P("mp"),
        P("mp", ("dp", "hidden")),
    )
    return jax.shard_map(
        local,
        mesh=mesh,
        in_specs=placed,
        out_specs=(
            P("mp", ("dp", "hidden")),
            P("mp", ("dp", "hidden")),
            P(None, ("mp", "dp", "hidden")),
            P(None, ("mp", "dp", "hidden")),
            P(("mp", "dp"), None, "hidden"),
            P(None, ("hidden", "dp")),
            P(("hidden", "dp"), "mp"),
            P(("mp", "dp")),
            P(("mp", "dp"), "hidden"),
            P(("hidden", "dp")),
            P(("mp", "dp"), "hidden"),
            P(("mp", "dp")),
        ),
        check_vma=False,
    )
```

time: 6500 us -> 707 us (0.11)
  waiting for transfers between devices: 4770 us -> 120 us
  matrix products: 436 us -> 0 us
  other arithmetic: 443 us -> 48.2 us
  local copies, waits for them, and re-layouts: 449 us -> 195 us
  blocking collectives: 342 us -> 116 us
  Pallas kernels: 0 us -> 187 us
    reduce_scatter x15 -> x1, waiting for transfers between devices: 3020 us -> 82.8 us  [local(): lax.psum_scatter(packed, GATHER, scatter_dimension=0, tiled=True)]
    all_gather x12 -> x1, waiting for transfers between devices: 1350 us -> 14.7 us  [local(): lax.all_gather(flat, GATHER, axis=0, tiled=True).reshape(hid, mp, dp, -1)]
    dot_general x33 -> x0, matrix products: 436 us -> none  [the longest x11 172 us: partial_term(): lax.dot_general(source, weight, (((1,), (contract,)), ((), ())), preferre...]
    all_to_all x3 -> x4, waiting for transfers between devices: 403 us -> 22.6 us  [the longest x1 22.6 us: local(): lax.all_to_all(out_t, 'mp', split_axis=0, concat_axis=1, tiled=True)]
    all_to_all x3 -> x0, blocking collectives: 219 us -> none  [from_heads(): lax.all_to_all(values, 'hidden', split_axis=2, concat_axis=0, tiled=True)]
    pallas_call x0 -> x5, Pallas kernels: none -> 187 us  [the longest x1 62.2 us: feed(): pl.pallas_call(feed_kernel, grid=(ff // FB,), in_specs=[whole((D, SEQ)),...]
    convert_element_type x27 -> x2, other arithmetic: 175 us -> 0.7 us  [the longest x1 0.69 us: position_table(): angles = rates[:, None] * positions.astype(F32)[None, :]]
    reduce_sum x12 -> x2, other arithmetic: 137 us -> 0.56 us  [local(): dg = jnp.stack([jnp.sum(dg_first, axis=2), jnp.sum(dg_second, axis=2)])]
  transfers between devices with their start and end apart: 31 -> 6, of which waited for: 25 -> 3; matrix products, arithmetic and copies ran while one was open for 8% -> 20% of each run, Pallas kernels for 0% -> 8%
where the time goes in v1:
time: 707 us; the launch traced here: 699 us
  local copies, waits for them, and re-layouts  195 us (28%)
  Pallas kernels  187 us (26%)
  waiting for transfers between devices  120 us (17%)
  blocking collectives  116 us (16%)
  other arithmetic  48.2 us (7%)
  starting transfers between devices  17.8 us (3%)
  between operations  15.3 us (2%)
    reduce_scatter x1, waiting for transfers between devices, local(): lax.psum_scatter(packed, GATHER, scatter_dimension=0, tiled=True)  82.8 us
    pallas_call x1, Pallas kernels, feed(): pl.pallas_call(feed_kernel, grid=(ff // FB,), in_specs=[whole((D, SEQ)),...  62.2 us
    psum x1, blocking collectives, local(): vectors = lax.psum(vectors, ('dp', 'mp', 'hidden'))  49.6 us
    pallas_call x1, Pallas kernels, attend_back(): pl.pallas_call(attend_back_kernel, grid=(PAIRS,), in_specs=[part(0), part...  48.1 us
    pallas_call x1, Pallas kernels, attend(): pl.pallas_call(attend_kernel, grid=(PAIRS,), in_specs=[part(0), part(1),...  42.7 us
    all_gather x2, blocking collectives, local(): lax.all_gather(t, 'mp', axis=1, tiled=True)  32.6 us
    concatenate x1, other arithmetic, local(): packed = jnp.concatenate([p1, p2, pe, pr], axis=1).reshape(-1, D)  31.7 us
    all_to_all x1, waiting for transfers between devices, local(): lax.all_to_all(out_t, 'mp', split_axis=0, concat_axis=1, tiled=True)  22.6 us
  transfers between devices with their start and end apart: 6, of which 3 were waited for; matrix products, arithmetic and copies ran while one was open for 20% of the time, Pallas kernels for 8%

profile of v1, /device:TPU:0, one launch (start us, length us, event | category | flops | bytes accessed | tf_op | source)
XLA Modules:
  0.0 699.4 jit_solution(15053173492490233729)
XLA Ops:
  11.3 1.3 copy.159
  12.6 5.3 all-to-all-start
  17.9 25.5 %all-gather = f32[4,192,2]{1,2,0:T(2,128)S(1)} all-gather(f32[1,192,2]{1,2,0:T(2,128)S(1)} %bitcast.124), channel_id=1, replica_groups=mesh['dp'=2,'mp'=4,'hidden'=4] {'mp'}, dimensions={0}, use_global_device_ids=true | all-gather | bytes 7680 | tf_op jit(solution)/shard_map/all_gather | solution.py:407
  44.5 11.4 %all-gather.2 = bf16[4,192,2]{1,2,0:T(2,128)(2,1)S(1)} all-gather(bf16[1,192,2]{1,2,0:T(2,128)(2,1)S(1)} %bitcast.126), channel_id=1, replica_groups=mesh['dp'=2,'mp'=4,'hidden'=4] {'hidden'}, dimensions={0}, use_global_device_ids=true | all-gather | bytes 3840 | tf_op jit(solution)/shard_map/all_gather | solution.py:409
  56.7 7.0 %all-gather.1 = f32[4,192,2]{1,2,0:T(2,128)S(1)} all-gather(f32[1,192,2]{1,2,0:T(2,128)S(1)} %bitcast.125), channel_id=1, replica_groups=mesh['dp'=2,'mp'=4,'hidden'=4] {'mp'}, dimensions={0}, use_global_device_ids=true | all-gather | bytes 7680 | tf_op jit(solution)/shard_map/all_gather | solution.py:407
  67.5 9.0 %all-reduce.2 = (bf16[768]{0:T(1024)(128)(2,1)S(1)}, bf16[768]{0:T(1024)(128)(2,1)S(1)}) all-reduce(bf16[768]{0:T(1024)(128)(2,1)S(1)} %dynamic-update-slice, bf16[768]{0:T(1024)(128)(2,1)S(1)} %dynamic-update-slice.1), channel_id=1, replica_groups=mesh['dp'=2,'mp'=4,'hidden'=4] {'mp'}, use_global_device_ids=true, to_apply=%add | all-reduce | flops 1536 | bytes 6144
  80.3 1.3 copy.158
  81.6 13.3 %all-gather.3 = bf16[4,1,768]{2,1,0:T(2,128)(2,1)S(1)} all-gather(bf16[1,1,768]{2,1,0:T(2,128)(2,1)S(1)} %reshape.218), channel_id=1, replica_groups=mesh['dp'=2,'mp'=4,'hidden'=4] {'hidden'}, dimensions={0}, use_global_device_ids=true | all-gather | bytes 7680 | tf_op jit(solution)/shard_map/all_gather | solution.py:410
  96.2 12.5 %fusion.tab_ref = f32[768,1024]{1,0:T(8,128)} fusion(f32[1024]{0:T(1024)S(1)} %dynamic-slice_convert_fusion, f32[768]{0:T(1024)S(1)} %fusion.3, pred[768]{0:T(1024)(128)(4,1)S(1)} %iota_compare_fusion), kind=kLoop, calls=%fused_computation.5 | loop fusion | flops 1572864 | bytes 3153664 | tf_op jit(solution)/shard_map/jit(_where)/select_n | solution.py:377
  108.8 14.7 %all-gather.6.cloned.1.call-done = bf16[9216,768]{1,0:T(8,128)(2,1)} async-done(((bf16[288,768]{1,0:T(8,128)(2,1)}), bf16[9216,768]{1,0:T(8,128)(2,1)}) %all-gather.6.cloned.1.call-update) | async-done | bytes 14155792 | tf_op jit(solution)/shard_map/all_gather | solution.py:400
  123.5 17.0 %reshape.180 = bf16[4,4,2,221184]{3,2,1,0:T(2,128)(2,1)} reshape(bf16[9216,768]{1,0:T(8,128)(2,1)} %all-gather.6.cloned.1.call-done) | data formatting | bytes 28311552 | tf_op jit(solution)/shard_map/reshape | solution.py:400
  140.5 4.4 all-to-all-start.1
  145.1 13.8 %fusion.7 = (bf16[4,4,2,73728]{3,2,1,0:T(2,128)(2,1)}, bf16[4,4,2,73728]{3,2,1,0:T(2,128)(2,1)}) fusion(bf16[4,4,2,221184]{3,2,1,0:T(2,128)(2,1)} %reshape.180), kind=kLoop, calls=%fused_computation.46 | loop fusion | bytes 18874368 | tf_op jit(solution)/shard_map/slice | solution.py:406
  158.9 4.2 slice.154
  163.1 13.2 %reshape.181 = bf16[4,768,3,192]{3,2,1,0:T(4,128)(2,1)} reshape(bf16[4,4,2,55296]{3,2,1,0:T(2,128)(2,1)} %slice.154) | data formatting | bytes 7077888 | tf_op jit(solution)/shard_map/reshape | solution.py:402
  176.2 9.9 %copy.117 = bf16[768,3,4,192]{0,3,2,1:T(8,128)(2,1)} copy(bf16[768,3,4,192]{3,1,0,2:T(4,128)(2,1)} %bitcast.94) | data formatting | bytes 7077888 | tf_op jit(solution)/shard_map/transpose | solution.py:402
  186.1 5.8 copy.121.w_ref
  191.9 11.5 %reshape.185 = bf16[4,768,768]{2,1,0:T(8,128)(2,1)} reshape(bf16[4,4,2,73728]{3,2,1,0:T(2,128)(2,1)} %get-tuple-element.107) | data formatting | bytes 9437184 | tf_op jit(solution)/shard_map/reshape | solution.py:405
  203.5 5.1 copy.146
  208.6 11.5 %reshape.187 = bf16[4,768,768]{2,1,0:T(8,128)(2,1)} reshape(bf16[4,4,2,73728]{3,2,1,0:T(2,128)(2,1)} %get-tuple-element.106) | data formatting | bytes 9437184 | tf_op jit(solution)/shard_map/reshape | solution.py:406
  220.1 5.2 copy.147
  225.3 1.8 reshape.183
  227.1 2.4 copy.124
  229.5 4.0 reshape.184.w2_ref
  233.6 14.4 %project.1 = (f32[768,1024]{1,0:T(8,128)}, bf16[768,1024]{1,0:T(8,128)(2,1)}, bf16[1024,2304]{1,0:T(8,128)(2,1)}) custom-call(bf16[768,1024]{1,0:T(8,128)(2,1)} %bitcast.106, f32[768,1024]{1,0:T(8,128)} %fusion.tab_ref, f32[768,1]{1,0:T(8,128)} %copy.119.g_ref, f32[768,1]{1,0:T(8,128)} %copy.120.b_ref, bf16[768,2304]{1,0:T(8,128)(2,1)} %copy.121.w_ref, ...), custom_call_target="tpu_custom_call" | custom-call | tf_op jit(solution)/shard_map/project/pallas_call | solution.py:78
  247.9 42.7 %attend.1 = (bf16[768,1024]{1,0:T(8,128)(2,1)}, f32[6,8,1024]{2,1,0:T(8,128)}) custom-call(bf16[1024,2304]{1,0:T(8,128)(2,1)} %get-tuple-element.33.q_ref.k_ref.v_ref, bf16[1024,2304]{1,0:T(8,128)(2,1)} %get-tuple-element.33.q_ref.k_ref.v_ref, bf16[1024,2304]{1,0:T(8,128)(2,1)} %get-tuple-element.33.q_ref.k_ref.v_ref, s32[1024,1]{1,0:T(8,128)} %copy.122.key_ref, ...), custom_call_target="tpu_custom_call" | custom-call | tf_op jit(solution)/shard_map/attend/pallas_call | solution.py:131
  290.6 62.2 %feed.1 = (bf16[768,1024]{1,0:T(8,128)(2,1)}, f32[768,1024]{1,0:T(8,128)}, bf16[1024,768]{1,0:T(8,128)(2,1)}, bf16[768,3072]{1,0:T(8,128)(2,1)}, bf16[768,3072]{...) custom-call(bf16[768,1024]{1,0:T(8,128)(2,1)} %get-tuple-element.34., ...), custom_call_target="tpu_custom_call" | custom-call | tf_op jit(solution)/shard_map/feed/pallas_call | solution.py:235
  352.8 48.1 %attend_back.1 = (bf16[768,1024]{1,0:T(8,128)(2,1)}, bf16[1024,768]{1,0:T(8,128)(2,1)}, bf16[1024,768]{1,0:T(8,128)(2,1)}) custom-call(bf16[1024,2304]{1,0:T(8,128)(2,1)} %get-tuple-element.33.q_ref.k_ref.v_ref, bf16[1024,2304]{1,0:T(8,128)(2,1)} %get-tuple-element.33.q_ref.k_ref.v_ref, bf16[1024,2304]{1,0:T(8,128)(2,1)} %get-tuple-element.33.q_ref.k_ref.v_ref, ...), custom_call_target="tpu_custom_call" | custom-call | tf_op jit(solution)/shard_map/attend_back/pallas_call | solution.py:296
  400.9 20.1 %project_back.1 = (bf16[768,2304]{1,0:T(8,128)(2,1)}, bf16[768,1024]{1,0:T(8,128)(2,1)}, f32[2,8,768]{2,1,0:T(8,128)}, f32[2,768,128]{2,1,0:T(8,128)}) custom-call(bf16[768,1024]{1,0:T(8,128)(2,1)} %get-tuple-element.37.ft_ref, bf16[768,1024]{1,0:T(8,128)(2,1)} %get-tuple-element.40.dqt_ref, bf16[1024,768]{1,0:T(8,128)(2,1)} %get-tuple-element.41.dk_ref, ...), custom_call_target="tpu_custom_call" | custom-call | tf_op jit(solution)/shard_map/project_back/pallas_call | solution.py:363
  421.0 5.8 copy.136
  426.8 9.9 %copy.137 = bf16[4,768,3,192]{3,2,1,0:T(4,128)(2,1)} copy(bf16[4,768,3,192]{1,3,0,2:T(8,128)(2,1)} %bitcast.102) | data formatting | bytes 7077888 | tf_op jit(solution)/shard_map/transpose | solution.py:430
  436.7 8.9 %reshape.192 = bf16[32,55296]{1,0:T(8,128)(2,1)} reshape(bf16[4,768,3,192]{3,2,1,0:T(4,128)(2,1)} %copy.137) | data formatting | bytes 7077888 | tf_op jit(solution)/shard_map/reshape | solution.py:430
  445.5 4.7 copy.157
  450.3 6.0 reshape.196
  456.3 4.8 copy.156
  461.1 6.2 reshape.198
  467.3 1.4 reshape.193
  469.0 1.7 reshape.194
  470.7 31.7 %pad_maximum_fusion = bf16[32,221184]{1,0:T(8,128)(2,1)} fusion(bf16[32,73728]{1,0:T(8,128)(2,1)} %reshape.198, bf16[32,73728]{1,0:T(8,128)(2,1)} %reshape.196, bf16[32,18432]{1,0:T(8,128)(2,1)S(1)} %reshape.194, bf16[32,55296]{1,0:T(8,128)(2,1)} %reshape.192), kind=kLoop, calls=%fused_computation | loop fusion | flops 56623104 | bytes 28311552 | tf_op jit(solution)/shard_map/concatenate | solution.py:434
  502.4 13.2 %reshape.199 = bf16[9216,768]{1,0:T(8,128)(2,1)} reshape(bf16[32,221184]{1,0:T(8,128)(2,1)} %pad_maximum_fusion) | data formatting | bytes 28311552 | tf_op jit(solution)/shard_map/reshape | solution.py:434
  515.7 4.2 all-to-all-start.3
  522.3 49.6 %psum.7 = f32[9216]{0:T(1024)S(1)} all-reduce(f32[9216]{0:T(1024)S(1)} %pad_maximum_fusion.2), channel_id=1, replica_groups=mesh['dp'=2,'mp'=4,'hidden'=4] {'dp','mp','hidden'}, use_global_device_ids=true, to_apply=%region_2.3 | all-reduce | flops 9216 | bytes 73728 | tf_op jit(solution)/shard_map/psum | solution.py:444
  571.9 3.6 all-to-all-start.2
  578.5 1.9 copy.149
  580.4 22.6 %all-to-all-done.2 = bf16[4,192,1024]{2,1,0:T(8,128)(2,1)S(1)} async-done(((bf16[4,192,1024]{2,1,0:T(8,128)(2,1)}), bf16[4,192,1024]{2,1,0:T(8,128)(2,1)S(1)}, u32[]{:S(2)}, u32[]{:S(2)}) %all-to-all-start.2) | async-done | bytes 1572896 | tf_op jit(solution)/shard_map/all_to_all | solution.py:426
  603.0 1.3 copy.148
  604.3 82.8 %reduce-scatter.2.cloned.1.call-done = bf16[288,768]{1,0:T(8,128)(2,1)} async-done(((bf16[9216,768]{1,0:T(8,128)(2,1)}), bf16[288,768]{1,0:T(8,128)(2,1)}) %reduce-scatter.2.cloned.1.call-update) | async-done | bytes 442384 | tf_op jit(solution)/shard_map/reduce_scatter | solution.py:435
  690.5 1.8 fusion.8
  (113 shorter events, 23.3 us)
Async XLA Ops:
  7.2 1.5 copy-start
  7.2 4.1 copy-start.4
  7.2 116.3 %all-gather.6.cloned.1.call-start = ((), (), s32[]{:S(2)}) async-start(), calls=%async_computation.5 | async-start | bytes 14598144 | tf_op jit(solution)/shard_map/all_gather | solution.py:400
  11.2 6.7 copy-start.12
  11.2 33.3 %copy-start.15 = (bf16[2,192]{1,0:T(2,128)(2,1)S(1)}, bf16[2,192]{1,0:T(2,128)(2,1)}, u32[]{:S(2)}) copy-start(bf16[2,192]{1,0:T(2,128)(2,1)} %param.22) | copy-start | bytes 2308
  11.2 45.4 %copy-start.13 = (f32[2,192]{1,0:T(2,128)S(1)}, f32[2,192]{1,0:T(2,128)}, u32[]{:S(2)}) copy-start(f32[2,192]{1,0:T(2,128)} %param.20) | copy-start | bytes 4612
  11.3 53.5 %copy-start.9 = (s32[1024]{0:T(1024)S(1)}, s32[1024]{0:T(1024)}, u32[]{:S(2)}) copy-start(s32[1024]{0:T(1024)} %param.17) | copy-start | bytes 12292
  11.3 53.5 %copy-start.11 = (s32[1024]{0:T(1024)S(1)}, s32[1024]{0:T(1024)}, u32[]{:S(2)}) copy-start(s32[1024]{0:T(1024)} %param.18) | copy-start | bytes 12292
  11.3 54.5 %copy-start.18 = (u32[32]{0:T(128)S(1)}, u32[32]{0:T(128)}, u32[]{:S(2)}) copy-start(u32[32]{0:T(128)} %constant.56) | copy-start | bytes 388
  11.3 55.8 %copy-start.16 = (bf16[192]{0:T(256)(128)(2,1)S(1)}, bf16[192]{0:T(256)(128)(2,1)}, u32[]{:S(2)}) copy-start(bf16[192]{0:T(256)(128)(2,1)} %param.24) | copy-start | bytes 1156
  11.3 56.0 %copy-start.17 = (bf16[192]{0:T(256)(128)(2,1)S(1)}, bf16[192]{0:T(256)(128)(2,1)}, u32[]{:S(2)}) copy-start(bf16[192]{0:T(256)(128)(2,1)} %param.28) | copy-start | bytes 1156
  12.6 67.7 %copy-start.5 = (bf16[192,4096]{1,0:T(8,128)(2,1)S(1)}, bf16[192,4096]{1,0:T(8,128)(2,1)}, u32[]{:S(2)}) copy-start(bf16[192,4096]{1,0:T(8,128)(2,1)} %param.29) | copy-start | bytes 4718596
  12.6 127.8 %all-to-all-start = ((bf16[192,4,1024]{2,0,1:T(8,128)(2,1)}), bf16[192,4,1024]{2,0,1:T(8,128)(2,1)S(1)}, u32[]{:S(2)}, u32[]{:S(2)}) async-start(bf16[192,4,1024]{2,0,1:T(8,128)(2,1)} %bitcast.92), calls=%async_computation | async-start | bytes 3145728 | tf_op jit(solution)/shard_map/all_to_all | solution.py:412
  17.9 63.7 %copy-start.14 = (bf16[768]{0:T(1024)(128)(2,1)S(1)}, bf16[768]{0:T(1024)(128)(2,1)}, u32[]{:S(2)}) copy-start(bf16[768]{0:T(1024)(128)(2,1)} %param.26) | copy-start | bytes 4612
  140.5 4.4 copy-start.3
  140.5 150.2 %all-to-all-start.1 = ((bf16[192,4,1024]{2,0,1:T(8,128)(2,1)}), bf16[192,4,1024]{2,0,1:T(8,128)(2,1)}, u32[]{:S(2)}, u32[]{:S(2)}) async-start(bf16[192,4,1024]{2,0,1:T(8,128)(2,1)} %bitcast.91), calls=%async_computation.1 | async-start | bytes 3145728 | tf_op jit(solution)/shard_map/all_to_all | solution.py:413
  144.8 542.3 %reduce-scatter.2.cloned.1.call-start = ((), (), s32[]{:S(2)}) async-start(), calls=%async_computation.6 | async-start | bytes 14598144 | tf_op jit(solution)/shard_map/reduce_scatter | solution.py:435
  145.1 13.8 %copy-start.2 = (bf16[4,4,2,221184]{3,2,1,0:T(2,128)(2,1)S(1)}, bf16[4,4,2,221184]{3,2,1,0:T(2,128)(2,1)}, u32[]{:S(2)}) copy-start(bf16[4,4,2,221184]{3,2,1,0:T(2,128)(2,1)} %reshape.180) | copy-start | bytes 42467332
  220.1 5.2 slice-start
  461.1 6.2 copy-start.6
  515.7 4.3 copy-start.8
  515.7 4.5 copy-start.7
  515.7 6.5 copy-start.10
  515.7 56.2 %all-to-all-start.3 = ((bf16[4,192,1024]{2,1,0:T(8,128)(2,1)}), bf16[4,192,1024]{2,1,0:T(8,128)(2,1)S(1)}, u32[]{:S(2)}, u32[]{:S(2)}) async-start(bf16[4,192,1024]{2,1,0:T(8,128)(2,1)} %bitcast.28), calls=%async_computation.3 | async-start | bytes 3145728 | tf_op jit(solution)/shard_map/all_to_all | solution.py:427
  571.9 31.1 %all-to-all-start.2 = ((bf16[4,192,1024]{2,1,0:T(8,128)(2,1)}), bf16[4,192,1024]{2,1,0:T(8,128)(2,1)S(1)}, u32[]{:S(2)}, u32[]{:S(2)}) async-start(bf16[4,192,1024]{2,1,0:T(8,128)(2,1)} %bitcast.112), calls=%async_computation.2 | async-start | bytes 3145728 | tf_op jit(solution)/shard_map/all_to_all | solution.py:426
  578.5 113.9 %copy-start.1 = (bf16[192,3,192]{2,0,1:T(8,128)(2,1)S(1)}, bf16[192,3,192]{2,0,1:T(8,128)(2,1)}, u32[]{:S(2)}) copy-start(bf16[192,3,192]{2,0,1:T(8,128)(2,1)} %param.21) | copy-start | bytes 663556
Sparse Core Ops, SparseCore 0:
  11.4 112.0 all-gather.5
  515.8 171.2 reduce-scatter.1

commit v2 on v1

--- a/solution.py
+++ b/solution.py
@@ -51,13 +51,19 @@
     return average, lax.rsqrt(spread + EPS)
 
 
-def project_kernel(x_ref, tab_ref, g_ref, b_ref, w_ref, wb_ref, et_ref, ft_ref, qkv_ref, f_ref):
+def project_kernel(x_ref, tab_ref, p_ref, wn_ref, wb_ref, et_ref, ft_ref, qkv_ref, w_ref, f_ref):
+    hid = wn_ref.shape[0]
+    wide = D // hid
+    for hh in range(hid):
+        for k in range(3):
+            w_ref[:, k * D + hh * wide : k * D + (hh + 1) * wide] = wn_ref[hh, :, k * wide : (k + 1) * wide]
+
     def norm_cols(j, _):
         cols = pl.ds(pl.multiple_of(j * 256, 256), 256)
         e = x_ref[:, cols].astype(F32) + tab_ref[:, cols]
         et_ref[:, cols] = e
         average, inv = norm_stats(e)
-        f = ((e - average) * inv * g_ref[...] + b_ref[...]).astype(BF16)
+        f = ((e - average) * inv * p_ref[:, 0:1] + p_ref[:, 1:2]).astype(BF16)
         ft_ref[:, cols] = f
         f_ref[cols, :] = f.T
         return 0
@@ -74,18 +80,19 @@
     lax.fori_loop(D // 256, 3 * D // 256, lambda n, c: cols_of(n, 1.0), 0)
 
 
-def project(xt, table, gain, shift, w1, bias_row):
+def project(xt, table, cols, w1, bias_row):
     return pl.pallas_call(
         project_kernel,
         out_shape=(
             jax.ShapeDtypeStruct((D, SEQ), F32),
             jax.ShapeDtypeStruct((D, SEQ), BF16),
             jax.ShapeDtypeStruct((SEQ, 3 * D), BF16),
+            jax.ShapeDtypeStruct((D, 3 * D), BF16),
         ),
         scratch_shapes=[pltpu.VMEM((SEQ, D), BF16)],
         compiler_params=params(),
         name="project",
-    )(xt, table, gain, shift, w1, bias_row)
+    )(xt, table, cols, w1, bias_row)
 
 
 def fill_bias(bias_ref, key_ref, seg_ref):
@@ -147,22 +154,26 @@
 
 
 def feed_kernel(
-    at_ref, et_ref, ct_ref, w2_ref, b2_ref, g_ref, b_ref, we_ref, be_ref, wr_ref, br_ref,
+    at_ref, et_ref, ct_ref, w2n_ref, p_ref, we_ref, be_ref, wr_ref,
     out_ref, dmid_ref, do_ref, dwr_ref, dwe_ref, dbe_ref, dw2_ref, db_ref, dg_ref,
-    s_ref, st_ref, c_ref, ot_ref, ds_ref, mid_ref, bt_ref,
+    s_ref, st_ref, c_ref, ot_ref, ds_ref, mid_ref, bt_ref, w2_ref,
 ):
     step = pl.program_id(0)
 
     @pl.when(step == 0)
     def _():
+        mp = w2n_ref.shape[0]
+        wide = D // mp
+        for j in range(mp):
+            w2_ref[:, j * wide : (j + 1) * wide] = w2n_ref[j]
         w2t = w2_ref[...].T
 
         def cols_of(j, _):
             cols = pl.ds(pl.multiple_of(j * 256, 256), 256)
-            mid = et_ref[:, cols] + (mm(w2t, at_ref[:, cols]) + b2_ref[...])
+            mid = et_ref[:, cols] + (mm(w2t, at_ref[:, cols]) + p_ref[:, 4:5])
             mid_ref[:, cols] = mid
             average, inv = norm_stats(mid)
-            s = ((mid - average) * inv * g_ref[...] + b_ref[...]).astype(BF16)
+            s = ((mid - average) * inv * p_ref[:, 2:3] + p_ref[:, 3:4]).astype(BF16)
             st_ref[:, cols] = s
             s_ref[cols, :] = s.T
             c_ref[cols, :] = ct_ref[:, cols].T
@@ -198,11 +209,11 @@
         def cols_of(j, _):
             cols = pl.ds(pl.multiple_of(j * 256, 256), 256)
             mid = mid_ref[:, cols]
-            out_ref[:, cols] = (mid + (ot_ref[:, cols] + br_ref[...])).astype(BF16)
+            out_ref[:, cols] = (mid + (ot_ref[:, cols] + p_ref[:, 5:6])).astype(BF16)
             average, inv = norm_stats(mid)
             normed = (mid - average) * inv
             ds = ds_ref[:, cols]
-            scaled = ds * g_ref[...]
+            scaled = ds * p_ref[:, 2:3]
             total = jnp.sum(scaled, axis=0, keepdims=True) * (1.0 / D)
             crossed = jnp.sum(scaled * normed, axis=0, keepdims=True) * (1.0 / D)
             dmid = ct_ref[:, cols].astype(F32) + inv * (scaled - total - normed * crossed)
@@ -219,15 +230,12 @@
         db_ref[0] = mm(ones, ct_ref[...], NT)
         db_ref[1] = mm(ones, bt_ref[...], NT)
 
-        def rows_of(j, _):
-            rows = pl.ds(pl.multiple_of(j * 256, 256), 256)
-            dw2_ref[rows, :] = mm(at_ref[rows, :], bt_ref[...], NT).astype(BF16)
-            return 0
-
-        lax.fori_loop(0, D // 256, rows_of, 0)
-
-
-def feed(at, et, ct, w2, b2, gain, shift, we, be, wr, br):
+        wide = D // dw2_ref.shape[0]
+        for j in range(dw2_ref.shape[0]):
+            dw2_ref[j] = mm(at_ref[...], bt_ref[j * wide : (j + 1) * wide, :], NT).astype(BF16)
+
+
+def feed(at, et, ct, w2, small, we, be, wr):
     ff = we.shape[1]
     cols = pl.BlockSpec((D, FB), lambda f: (0, f))
     row = pl.BlockSpec((1, FB), lambda f: (0, f))
@@ -236,25 +244,24 @@
         feed_kernel,
         grid=(ff // FB,),
         in_specs=[
-            whole((D, SEQ)), whole((D, SEQ)), whole((D, SEQ)), whole((D, D)), whole((D, 1)), whole((D, 1)),
-            whole((D, 1)), cols, row, cols, whole((D, 1)),
+            whole((D, SEQ)), whole((D, SEQ)), whole((D, SEQ)), whole(w2.shape), whole((D, 128)), cols, row, cols,
         ],
         out_specs=(
-            whole((D, SEQ)), whole((D, SEQ)), whole((SEQ, D)), cols, cols, row, whole((D, D)),
+            whole((D, SEQ)), whole((D, SEQ)), whole((SEQ, D)), cols, cols, row, whole(w2.shape),
             whole((2, 8, D)), whole((2, D, 128)),
         ),
         out_shape=(
             sds((D, SEQ), BF16), sds((D, SEQ), F32), sds((SEQ, D), BF16), sds((D, ff), BF16), sds((D, ff), BF16),
-            sds((1, ff), F32), sds((D, D), BF16), sds((2, 8, D), F32), sds((2, D, 128), F32),
+            sds((1, ff), F32), sds(w2.shape, BF16), sds((2, 8, D), F32), sds((2, D, 128), F32),
         ),
         scratch_shapes=[
             pltpu.VMEM((SEQ, D), BF16), pltpu.VMEM((D, SEQ), BF16), pltpu.VMEM((SEQ, D), BF16),
             pltpu.VMEM((D, SEQ), F32), pltpu.VMEM((D, SEQ), F32), pltpu.VMEM((D, SEQ), F32),
-            pltpu.VMEM((D, SEQ), BF16),
+            pltpu.VMEM((D, SEQ), BF16), pltpu.VMEM((D, D), BF16),
         ],
         compiler_params=params(),
         name="feed",
-    )(at, et, ct, w2, b2, gain, shift, we, be, wr, br)
+    )(at, et, ct, w2, small, we, be, wr)
 
 
 def attend_back_kernel(
@@ -316,8 +323,8 @@
 
 
 def project_back_kernel(
-    ft_ref, dqt_ref, dk_ref, dv_ref, w_ref, et_ref, dmid_ref, g_ref,
-    dw_ref, dx_ref, db_ref, dg_ref, df_ref,
+    ft_ref, dqt_ref, dk_ref, dv_ref, w_ref, et_ref, dmid_ref, p_ref,
+    dwn_ref, dx_ref, db_ref, dg_ref, df_ref, dw_ref,
 ):
     df_ref[...] = jnp.zeros_like(df_ref)
 
@@ -336,6 +343,11 @@
         return 0
 
     lax.fori_loop(0, D // 256, cols_of, 0)
+    hid = dwn_ref.shape[0]
+    wide = D // hid
+    for hh in range(hid):
+        for k in range(3):
+            dwn_ref[hh, :, k * wide : (k + 1) * wide] = dw_ref[:, k * D + hh * wide : k * D + (hh + 1) * wide]
     ones = jnp.ones((8, SEQ), BF16)
     db_ref[0] = mm(ones, dqt_ref[...], NT)
     db_ref[1] = mm(ones, dv_ref[...])
@@ -347,7 +359,7 @@
         average, inv = norm_stats(e)
         normed = (e - average) * inv
         df = df_ref[:, cols]
-        scaled = df * g_ref[...]
+        scaled = df * p_ref[:, 0:1]
         total = jnp.sum(scaled, axis=0, keepdims=True) * (1.0 / D)
         crossed = jnp.sum(scaled * normed, axis=0, keepdims=True) * (1.0 / D)
         dx_ref[:, cols] = (dmid_ref[:, cols] + inv * (scaled - total - normed * crossed)).astype(BF16)
@@ -358,15 +370,17 @@
     lax.fori_loop(0, SEQ // 256, norm_cols, 0)
 
 
-def project_back(ft, dqt, dk, dv, w1, et, dmid, gain):
+def project_back(ft, dqt, dk, dv, w1, et, dmid, cols, hid):
     sds = jax.ShapeDtypeStruct
     return pl.pallas_call(
         project_back_kernel,
-        out_shape=(sds((D, 3 * D), BF16), sds((D, SEQ), BF16), sds((2, 8, D), F32), sds((2, D, 128), F32)),
-        scratch_shapes=[pltpu.VMEM((D, SEQ), F32)],
+        out_shape=(
+            sds((hid, D, 3 * D // hid), BF16), sds((D, SEQ), BF16), sds((2, 8, D), F32), sds((2, D, 128), F32)
+        ),
+        scratch_shapes=[pltpu.VMEM((D, SEQ), F32), pltpu.VMEM((D, 3 * D), BF16)],
         compiler_params=params(),
         name="project_back",
-    )(ft, dqt, dk, dv, w1, et, dmid, gain)
+    )(ft, dqt, dk, dv, w1, et, dmid, cols)
 
 
 def position_table(positions):
@@ -377,7 +391,332 @@
     return jnp.where(rows[:, None] < half, jnp.sin(angles), jnp.cos(angles))
 
 
-GATHER = ("hidden", "mp", "dp")
+MESH = pl.DeviceIdType.MESH
+
+
+class Wire:
+    def __init__(self, send, recv):
+        self.send_sem, self.recv_sem, self.count, self.sent = send, recv, 0, []
+        self.me = (lax.axis_index("dp"), lax.axis_index("mp"), lax.axis_index("hidden"))
+        self.size = (lax.axis_size("dp"), lax.axis_size("mp"), lax.axis_size("hidden"))
+
+    def peer(self, axis, offset):
+        where = list(self.me)
+        where[axis] = lax.rem(where[axis] + offset, self.size[axis])
+        return tuple(where)
+
+    def origin(self, axis, offset):
+        return lax.rem(self.me[axis] - offset + self.size[axis], self.size[axis])
+
+    def meet(self):
+        barrier = pltpu.get_barrier_semaphore()
+        total = 0
+        for axis in range(3):
+            for offset in range(1, self.size[axis]):
+                pl.semaphore_signal(barrier, 1, device_id=self.peer(axis, offset), device_id_type=MESH)
+                total += 1
+        pl.semaphore_wait(barrier, total)
+
+    def send(self, src, dst, target):
+        copy = pltpu.make_async_remote_copy(
+            src, dst, self.send_sem.at[self.count], self.recv_sem.at[self.count], device_id=target, device_id_type=MESH
+        )
+        copy.start()
+        self.count += 1
+        self.sent.append(copy)
+        return copy
+
+    def keep(self, src, dst):
+        copy = pltpu.make_async_copy(src, dst, self.send_sem.at[self.count])
+        copy.start()
+        self.count += 1
+        return copy
+
+    def finish(self):
+        for copy in self.sent:
+            copy.wait_send()
+
+
+DP, MP, HID = 0, 1, 2
+
+
+def gather_kernel(
+    n_sems, x_ref, c_ref, w1_ref, w2_ref, we_ref, wr_ref, cols_ref, rows_ref,
+    xt_ref, ct_ref, w1f_ref, w2f_ref, wef_ref, wrf_ref, colsf_ref, rowsf_ref, send, recv,
+):
+    wire = Wire(send, recv)
+    d, m, h = wire.me
+    dp, mp, hid = wire.size
+    rows = D // mp
+    fcols = we_ref.shape[1]
+    half = rows // dp
+    offset = pl.multiple_of(d * half, half)
+    own = (
+        (w1_ref, lambda mm_, hh: w1f_ref.at[hh, mm_, d], w1f_ref.at[:, :, d]),
+        (w2_ref, lambda mm_, hh: w2f_ref.at[mm_, hh, d], w2f_ref.at[:, :, d]),
+        (we_ref.at[pl.ds(offset, half)], lambda mm_, hh: wef_ref.at[mm_, d, :, pl.ds(pl.multiple_of(hh * fcols, fcols), fcols)], wef_ref.at[:, d]),
+        (wr_ref.at[pl.ds(offset, half)], lambda mm_, hh: wrf_ref.at[mm_, d, :, pl.ds(pl.multiple_of(hh * fcols, fcols), fcols)], wrf_ref.at[:, d]),
+    )
+    wire.meet()
+    waits = []
+    local = []
+
+    def swap(src_ref, dst_ref):
+        mine = pl.ds(pl.multiple_of(m * rows, rows), rows)
+        for q in range(1, mp):
+            to = wire.peer(MP, q)
+            waits.append(wire.send(src_ref.at[:, pl.ds(pl.multiple_of(to[1] * SEQ, SEQ), SEQ)], dst_ref.at[mine], to))
+        local.append(wire.keep(src_ref.at[:, pl.ds(pl.multiple_of(m * SEQ, SEQ), SEQ)], dst_ref.at[mine]))
+
+    for q in range(1, mp):
+        waits.append(wire.send(cols_ref, colsf_ref.at[pl.ds(pl.multiple_of(m * rows, rows), rows)], wire.peer(MP, q)))
+    local.append(wire.keep(cols_ref, colsf_ref.at[pl.ds(pl.multiple_of(m * rows, rows), rows)]))
+    for o in range(1, hid):
+        waits.append(wire.send(rows_ref, rowsf_ref.at[h], wire.peer(HID, o)))
+    local.append(wire.keep(rows_ref, rowsf_ref.at[h]))
+
+    first = {}
+
+    def stage_one(i, axis):
+        src, dst, _ = own[i]
+        first[i] = [wire.send(src, dst(m, h), wire.peer(axis, o)) for o in range(1, wire.size[axis])]
+        first[i].insert(0, wire.keep(src, dst(m, h)))
+
+    second = {}
+
+    def stage_two(i, axis):
+        _, dst, _ = own[i]
+        other = MP if axis == HID else HID
+        second[i] = []
+        for o, copy in enumerate(first[i]):
+            if o == 0:
+                copy.wait()
+            else:
+                copy.wait_recv()
+            at = wire.origin(axis, o)
+            piece = dst(m, at) if axis == HID else dst(at, h)
+            second[i] += [wire.send(piece, piece, wire.peer(other, q)) for q in range(1, wire.size[other])]
+
+    def stage_three(i):
+        slab = own[i][2]
+        for copy in second[i]:
+            copy.wait_recv()
+        for r in range(1, dp):
+            waits.append(wire.send(slab, slab, wire.peer(DP, r)))
+
+    routes = (HID, HID, HID, MP)
+    stage_one(0, routes[0])
+    swap(x_ref, xt_ref)
+    for i in (1, 2, 3):
+        stage_one(i, routes[i])
+    swap(c_ref, ct_ref)
+    for i in range(4):
+        stage_two(i, routes[i])
+    for i in range(4):
+        stage_three(i)
+    for copy in local:
+        copy.wait()
+    for copy in waits:
+        copy.wait_recv()
+    wire.finish()
+
+
+def gather(x, c, w1, w2, we, wr, cols, rows):
+    dp, mp, hid = lax.axis_size("dp"), lax.axis_size("mp"), lax.axis_size("hidden")
+    half = D // mp // dp
+    fcols = we.shape[1]
+    sds = jax.ShapeDtypeStruct
+    out_shape = (
+        sds((D, SEQ), BF16), sds((D, SEQ), BF16), sds((hid, mp, dp, half, w1.shape[1]), BF16),
+        sds((mp, hid, dp) + w2.shape, BF16), sds((mp, dp, half, hid * fcols), BF16),
+        sds((mp, dp, half, hid * fcols), BF16), sds((D, cols.shape[1]), F32), sds((hid,) + rows.shape, F32),
+    )
+    n = 3 * mp + hid + 4 * (hid + mp + hid * mp + dp) + 8
+    hbm = pl.BlockSpec(memory_space=pl.ANY)
+    return pl.pallas_call(
+        functools.partial(gather_kernel, n),
+        out_shape=out_shape,
+        in_specs=[hbm] * 8,
+        out_specs=(hbm,) * 8,
+        scratch_shapes=[pltpu.SemaphoreType.DMA((n,)), pltpu.SemaphoreType.DMA((n,))],
+        compiler_params=params(collective_id=0, has_side_effects=True),
+        name="gather",
+    )(x, c, w1, w2, we, wr, cols, rows)
+
+
+def scatter_kernel(
+    o_ref, x_ref, dw1_ref, dw2_ref, dwe_ref, dwr_ref, vec_ref,
+    of_ref, xf_ref, g1_ref, g2_ref, ge_ref, gr_ref, vecf_ref,
+    a1, a2, ae, ar, s1, s2, se, sr, b1, b2, be, br, t1, t2, te, tr, c1, c2, ce, cr, va, vb, vc, v1, v2, send, recv,
+):
+    wire = Wire(send, recv)
+    v_in = (va, vb, vc)
+    d, m, h = wire.me
+    dp, mp, hid = wire.size
+    rows = D // mp
+    fcols = ge_ref.shape[1]
+    waits, local = [], []
+    wire.meet()
+    hslice = lambda hh: pl.ds(pl.multiple_of(hh * fcols, fcols), fcols)
+    items = (
+        (lambda dd: dw1_ref.at[:, :, dd], a1, s1, b1, t1, c1, g1_ref, HID, MP),
+        (lambda dd: dw2_ref.at[:, :, dd], a2, s2, b2, t2, c2, g2_ref, MP, HID),
+        (lambda dd: dwe_ref.at[:, dd], ae, se, be, te, ce, ge_ref, None, MP),
+        (lambda dd: dwr_ref.at[:, dd], ar, sr, br, tr, cr, gr_ref, None, HID),
+    )
+    core = {}
+    loads = {}
+
+    def stage_core(i):
+        src, a, s = items[i][:3]
+        core[i] = [wire.send(src(wire.peer(DP, r)[0]), a.at[r - 1], wire.peer(DP, r)) for r in range(1, dp)]
+        loads[i] = wire.keep(src(d), s)
+
+    def swap(src_ref, dst_ref):
+        mine = pl.ds(pl.multiple_of(m * SEQ, SEQ), SEQ)
+        for q in range(1, mp):
+            to = wire.peer(MP, q)
+            waits.append(wire.send(src_ref.at[pl.ds(pl.multiple_of(to[1] * rows, rows), rows)], dst_ref.at[:, mine], to))
+        local.append(wire.keep(src_ref.at[pl.ds(pl.multiple_of(m * rows, rows), rows)], dst_ref.at[:, mine]))
+
+    def add_all(dst, own, others, shape):
+        lead = shape[:-2]
+        total = math.prod(lead)
+
+        def body(n, _):
+            index = []
+            for size in reversed(lead):
+                index.insert(0, lax.rem(n, size))
+                n = lax.div(n, size)
+            index = tuple(index)
+            value = own[index].astype(F32)
+            for j in range(others.shape[0]):
+                value = value + others[(j,) + index].astype(F32)
+            dst[index] = value.astype(dst.dtype)
+            return 0
+
+        lax.fori_loop(0, total, body, 0)
+
+    def part(i, ref, axis, at):
+        if i < 2:
+            lead = items[i][7] == axis
+            return ref.at[at] if lead else ref.at[:, at]
+        return ref.at[at] if axis == MP else ref.at[:, :, hslice(at)]
+
+    plane = {}
+
+    def stage_plane(i):
+        _, a, s, b, t, c, g, _, axis = items[i]
+        for copy in core[i]:
+            copy.wait_recv()
+        loads[i].wait()
+        add_all(s, s, a, s.shape)
+        plane[i] = [
+            wire.send(part(i, s, axis, wire.peer(axis, q)[axis]), b.at[q - 1], wire.peer(axis, q))
+            for q in range(1, wire.size[axis])
+        ]
+
+    last = {}
+
+    def stage_last(i):
+        _, a, s, b, t, c, g, _, axis = items[i]
+        for copy in plane[i]:
+            copy.wait_recv()
+        add_all(t, part(i, s, axis, wire.me[axis]), b, t.shape)
+        other = MP if axis == HID else HID
+        last[i] = []
+        for q in range(1, wire.size[other]):
+            to = wire.peer(other, q)
+            if i < 2 or other == MP:
+                src = t.at[to[other]]
+            else:
+                src = t.at[:, hslice(to[other])]
+            last[i].append(wire.send(src, c.at[q - 1], to))
+
+    def stage_end(i):
+        _, a, s, b, t, c, g, _, axis = items[i]
+        other = MP if axis == HID else HID
+        for copy in last[i]:
+            copy.wait_recv()
+        own = t[wire.me[other]] if (i < 2 or other == MP) else t[:, hslice(h)]
+        value = own.astype(F32)
+        for j in range(c.shape[0]):
+            value = value + c[j].astype(F32)
+        g[...] = value
+
+    vec = {}
+
+    def vec_send(axis, src):
+        vec[axis] = [wire.send(src, v_in[axis].at[o - 1], wire.peer(axis, o)) for o in range(1, wire.size[axis])]
+
+    def vec_sum(axis, src, dst):
+        for copy in vec[axis]:
+            copy.wait_recv()
+        total = src[...]
+        for j in range(wire.size[axis] - 1):
+            total = total + v_in[axis][j]
+        dst[...] = total
+
+    vec_send(DP, vec_ref)
+    for i in (3, 2, 1, 0):
+        stage_core(i)
+    swap(o_ref, of_ref)
+    for i in (3, 2, 1, 0):
+        stage_plane(i)
+    swap(x_ref, xf_ref)
+    vec_sum(DP, vec_ref, v1)
+    vec_send(MP, v1)
+    for i in (3, 2, 1, 0):
+        stage_last(i)
+    vec_sum(MP, v1, v2)
+    vec_send(HID, v2)
+    for i in (3, 2, 1, 0):
+        stage_end(i)
+    vec_sum(HID, v2, vecf_ref)
+    for copy in local:
+        copy.wait()
+    for copy in waits:
+        copy.wait_recv()
+    wire.finish()
+
+
+def scatter(o, x, dw1, dw2, dwe, dwr, vec):
+    dp, mp, hid = lax.axis_size("dp"), lax.axis_size("mp"), lax.axis_size("hidden")
+    sds = jax.ShapeDtypeStruct
+    half, c1 = dw1.shape[3:]
+    half2, c2 = dw2.shape[3:]
+    ff = dwe.shape[3]
+    fc = ff // hid
+    out_shape = (
+        sds((D // mp, mp * SEQ), BF16), sds((D // mp, mp * SEQ), BF16), sds((half, c1), F32), sds((half2, c2), F32),
+        sds((half, fc), F32), sds((half, fc), F32), sds(vec.shape, F32),
+    )
+    vm = lambda *shape: pltpu.VMEM(shape, BF16)
+    slabs = ((hid, mp, half, c1), (mp, hid, half2, c2), (mp, half, ff), (mp, half, ff))
+    after = ((hid, half, c1), (mp, half2, c2), (half, ff), (mp, half, fc))
+    ends = ((half, c1), (half2, c2), (half, fc), (half, fc))
+    near = (mp, hid, mp, hid)
+    far = (hid, mp, hid, mp)
+    scratch = [vm(dp - 1, *s) for s in slabs] + [vm(*s) for s in slabs]
+    scratch += [vm(n - 1, *s) for n, s in zip(near, after)] + [vm(*s) for s in after]
+    scratch += [vm(n - 1, *s) for n, s in zip(far, ends)]
+    scratch += [
+        pltpu.VMEM((dp - 1,) + vec.shape, F32), pltpu.VMEM((mp - 1,) + vec.shape, F32),
+        pltpu.VMEM((hid - 1,) + vec.shape, F32), pltpu.VMEM(vec.shape, F32), pltpu.VMEM(vec.shape, F32),
+    ]
+    n = dp + mp + hid + 2 * mp + 4 * (dp + mp + hid + 1) + 8
+    scratch += [pltpu.SemaphoreType.DMA((n,)), pltpu.SemaphoreType.DMA((n,))]
+    hbm = pl.BlockSpec(memory_space=pl.ANY)
+    vmem = pl.BlockSpec(memory_space=pltpu.VMEM)
+    return pl.pallas_call(
+        scatter_kernel,
+        out_shape=out_shape,
+        in_specs=[hbm] * 6 + [vmem],
+        out_specs=(hbm, hbm) + (vmem,) * 5,
+        scratch_shapes=scratch,
+        compiler_params=params(collective_id=1, has_side_effects=True),
+        name="scatter",
+    )(o, x, dw1, dw2, dwe, dwr, vec)
 
 
 def local(
@@ -385,74 +724,64 @@
     output_bias, expand_weight, expand_bias, reduce_weight, reduce_bias, cotangent,
 ):
     mp, hid, dp = lax.axis_size("mp"), lax.axis_size("hidden"), lax.axis_size("dp")
-    m = lax.axis_index("mp")
-    d = lax.axis_index("dp")
-    rows_mp = D // mp
+    m, h, d = lax.axis_index("mp"), lax.axis_index("hidden"), lax.axis_index("dp")
+    rows_mp, hcols, fcols = D // mp, D // hid, expand_weight.shape[1]
     half = rows_mp // dp
-    cut = lambda w: lax.dynamic_slice_in_dim(w, d * half, half, 0)
-    hcols = D // hid
-    w1 = cut(input_proj).reshape(-1)
-    we = cut(expand_weight).reshape(-1)
-    wr = cut(reduce_weight).reshape(-1)
-    w2 = lax.dynamic_slice_in_dim(output_proj, d * (hcols // dp), hcols // dp, 0).reshape(-1)
-    sizes = [w1.size, w2.size, we.size, wr.size]
-    flat = jnp.concatenate([w1, w2, we, wr]).reshape(-1, D)
-    full = lax.all_gather(flat, GATHER, axis=0, tiled=True).reshape(hid, mp, dp, -1)
-    o0, o1, o2 = sizes[0], sizes[0] + sizes[1], sizes[0] + sizes[1] + sizes[2]
-    w1f = full[..., :o0].reshape(hid, D, 3, hcols).transpose(1, 2, 0, 3).reshape(D, 3 * D)
-    w2f = full[..., o0:o1].reshape(hid, mp, dp, hcols // dp, rows_mp).transpose(0, 2, 3, 1, 4).reshape(D, D)
-    fcols = expand_weight.shape[1]
-    wef = full[..., o1:o2].reshape(hid, D, fcols).transpose(1, 0, 2).reshape(D, -1)
-    wrf = full[..., o2:].reshape(hid, D, fcols).transpose(1, 0, 2).reshape(D, -1)
-    gains, shifts = (lax.all_gather(t, "mp", axis=1, tiled=True) for t in (norm_gains, norm_biases))
-    b2, br = (lax.all_gather(t, "mp", axis=0, tiled=True).astype(F32)[:, None] for t in (output_bias, reduce_bias))
-    b1 = lax.all_gather(input_bias, "hidden", axis=1, tiled=True).astype(F32)
-    be = lax.all_gather(expand_bias, "hidden", axis=0, tiled=True).astype(F32)[None]
+    cols = [norm_gains[0], norm_biases[0], norm_gains[1], norm_biases[1], output_bias.astype(F32), reduce_bias.astype(F32)]
+    cols = jnp.pad(jnp.stack(cols, axis=1), ((0, 0), (0, 128 - len(cols))))
+    rows = jnp.concatenate(
+        [
+            expand_bias.astype(F32)[None],
+            jnp.pad(input_bias.astype(F32), ((0, 0), (0, fcols - hcols))),
+            jnp.zeros((5, fcols), F32),
+        ]
+    )
+    w1 = lax.dynamic_slice_in_dim(input_proj, d * half, half, 0).reshape(half, 3 * hcols)
+    w2 = lax.dynamic_slice_in_dim(output_proj, d * (hcols // dp), hcols // dp, 0)
+    xt, ct, w1n, w2n, we, wr, cols, rows = gather(
+        stored, cotangent, w1, w2, expand_weight, reduce_weight, cols, rows
+    )
+    w1n = w1n.reshape(hid, D, 3 * hcols)
+    w2n = w2n.reshape(mp, D, rows_mp)
+    we, wr = we.reshape(D, hid * fcols), wr.reshape(D, hid * fcols)
+    be = rows[:, 0].reshape(1, hid * fcols)
+    b1 = rows[:, 1:3, :hcols].transpose(1, 0, 2).reshape(2, D)
     bias_row = jnp.concatenate([b1[0], jnp.zeros_like(b1[0]), b1[1]])[None]
-    xt = lax.all_to_all(stored, "mp", split_axis=1, concat_axis=0, tiled=True)
-    ct = lax.all_to_all(cotangent, "mp", split_axis=1, concat_axis=0, tiled=True)
+
     table = position_table(lax.dynamic_slice_in_dim(positions, m * SEQ, SEQ))
     key_col = jnp.where(present == 1, segments, -1)[:, None]
     seg_row = segments[None, :]
 
-    et, ft, qkv = project(xt, table, gains[0][:, None], shifts[0][:, None], w1f, bias_row)
+    et, ft, qkv, w1f = project(xt, table, cols, w1n, bias_row)
     at, lse = attend(qkv, key_col, seg_row)
-    out_t, dmid, do, dwr, dwe, dbe, dw2, db_feed, dg_second = feed(
-        at, et, ct, w2f, b2, gains[1][:, None], shifts[1][:, None], wef, be, wrf, br
-    )
+    out_t, dmid, do, dwr, dwe, dbe, dw2, db_feed, dg_second = feed(at, et, ct, w2n, cols, we, be, wr)
     dqt, dk, dv = attend_back(qkv, do, lse, key_col, seg_row)
-    dw1, dx, db_proj, dg_first = project_back(ft, dqt, dk, dv, w1f, et, dmid, gains[0][:, None])
-
-    output = lax.all_to_all(out_t, "mp", split_axis=0, concat_axis=1, tiled=True)
-    d_stored = lax.all_to_all(dx, "mp", split_axis=0, concat_axis=1, tiled=True).astype(F32)
-
-    n_parts = hid * mp * dp
-    p1 = dw1.reshape(D, 3, hid, hcols).transpose(2, 0, 1, 3).reshape(n_parts, -1)
-    p2 = dw2.reshape(hid, dp, hcols // dp, mp, rows_mp).transpose(0, 3, 1, 2, 4).reshape(n_parts, -1)
-    pe = dwe.reshape(D, hid, fcols).transpose(1, 0, 2).reshape(n_parts, -1)
-    pr = dwr.reshape(D, hid, fcols).transpose(1, 0, 2).reshape(n_parts, -1)
-    packed = jnp.concatenate([p1, p2, pe, pr], axis=1).reshape(-1, D)
-    mine = lax.psum_scatter(packed, GATHER, scatter_dimension=0, tiled=True).reshape(-1).astype(F32)
-    d_input = mine[:o0].reshape(half, 3, hcols)
-    d_output = mine[o0:o1].reshape(hcols // dp, rows_mp)
-    d_expand = mine[o1:o2].reshape(half, fcols)
-    d_reduce = mine[o2:].reshape(half, fcols)
+    dw1, dx, db_proj, dg_first = project_back(ft, dqt, dk, dv, w1f, et, dmid, cols, hid)
+
     dg = jnp.stack([jnp.sum(dg_first, axis=2), jnp.sum(dg_second, axis=2)])
     vectors = jnp.concatenate(
         [dg.reshape(-1), db_proj[:, 0].reshape(-1), db_feed[:, 0].reshape(-1), dbe.reshape(-1)]
-    )
-    vectors = lax.psum(vectors, ("dp", "mp", "hidden"))
-    h = lax.axis_index("hidden")
+    ).reshape(-1, 128)
+    output, d_stored, d_input, d_output, d_expand, d_reduce, vectors = scatter(
+        out_t,
+        dx,
+        dw1.reshape(hid, mp, dp, half, 3 * hcols),
+        dw2.reshape(mp, hid, dp, hcols // dp, rows_mp),
+        dwe.reshape(mp, dp, half, hid * fcols),
+        dwr.reshape(mp, dp, half, hid * fcols),
+        vectors,
+    )
+    vectors = vectors.reshape(-1)
     dg = vectors[: 4 * D].reshape(2, 2, D)
-    piece = D // n_parts
+    piece = D // (hid * mp * dp)
     dg = lax.dynamic_slice_in_dim(dg, ((m * dp + d) * hid + h) * piece, piece, 2)
     db_proj = vectors[4 * D : 6 * D].reshape(2, D)
     db_proj = lax.dynamic_slice_in_dim(db_proj, (h * dp + d) * (hcols // dp), hcols // dp, 1)
     db_feed = lax.dynamic_slice_in_dim(vectors[6 * D : 8 * D].reshape(2, D), (m * dp + d) * half, half, 1)
     dbe = lax.dynamic_slice_in_dim(vectors[8 * D :], (h * dp + d) * (fcols // dp), fcols // dp)
     return (
-        output, d_stored, dg[:, 0], dg[:, 1], d_input, db_proj, d_output, db_feed[1], d_expand, dbe, d_reduce,
-        db_feed[0],
+        output, d_stored.astype(F32), dg[:, 0], dg[:, 1], d_input.reshape(half, 3, hcols), db_proj, d_output, db_feed[1],
+        d_expand, dbe, d_reduce, db_feed[0],
     )
 
 

time: 707 us -> 452 us (0.64); the launches traced: 699 us -> 452 us
  Pallas kernels: 187 us -> 411 us
  local copies, waits for them, and re-layouts: 195 us -> 18.3 us
  waiting for transfers between devices: 120 us -> 0 us
  blocking collectives: 116 us -> 0 us
  other arithmetic: 48.2 us -> 21.9 us
  starting transfers between devices: 17.8 us -> 0 us
  between operations: 15.3 us -> 0.83 us
    pallas_call x1 -> x3, Pallas kernels: 20.1 us -> 242 us  [the longest x1 117 us: gather(): pl.pallas_call(functools.partial(gather_kernel, n), out_shape=out_shape,...]
    reshape x23 -> x4, local copies, waits for them, and re-layouts: 124 us -> 0.83 us  [the longest x1 0.79 us: local(): lax.dynamic_slice_in_dim(input_proj, d * half, half, 0)]
    reduce_scatter x1 -> x0, waiting for transfers between devices: 82.8 us -> none  [local(): lax.psum_scatter(packed, GATHER, scatter_dimension=0, tiled=True)]
    all_gather x4 -> x0, blocking collectives: 57.2 us -> none  [the longest x2 32.6 us: local(): lax.all_gather(t, 'mp', axis=1, tiled=True)]
    psum x1 -> x0, blocking collectives: 49.6 us -> none  [local(): vectors = lax.psum(vectors, ('dp', 'mp', 'hidden'))]
    concatenate x3 -> x1, other arithmetic: 31.7 us -> 0.68 us  [local(): jnp.concatenate([expand_bias.astype(F32)[None], jnp.pad(input_bias.astype...]
    all_to_all x4 -> x0, waiting for transfers between devices: 22.6 us -> none  [the longest x1 22.6 us: local(): lax.all_to_all(out_t, 'mp', split_axis=0, concat_axis=1, tiled=True)]
    transpose x3 -> x1, local copies, waits for them, and re-layouts: 22.2 us -> 0.76 us  [local(): b1 = rows[:, 1:3, :hcols].transpose(1, 0, 2).reshape(2, D)]
  transfers between devices with their start and end apart: 6 -> 0, of which waited for: 3 -> 0; matrix products, arithmetic and copies ran while one was open for 20% -> 0% of each run, Pallas kernels for 8% -> 0%
where the time goes in v2:
time: 452 us
  Pallas kernels  411 us (91%)
  other arithmetic  21.9 us (5%)
  local copies, waits for them, and re-layouts  18.3 us (4%)
    pallas_call x1, Pallas kernels, gather(): pl.pallas_call(functools.partial(gather_kernel, n), out_shape=out_shape,...  117 us
    pallas_call x1, Pallas kernels, scatter(): pl.pallas_call(scatter_kernel, out_shape=out_shape, in_specs=[hbm] * 6 +...  106 us
    pallas_call x1, Pallas kernels, feed(): pl.pallas_call(feed_kernel, grid=(ff // FB,), in_specs=[whole((D, SEQ)),...  61.3 us
    pallas_call x1, Pallas kernels, attend_back(): pl.pallas_call(attend_back_kernel, grid=(PAIRS,), in_specs=[part(0), part...  48.1 us
    pallas_call x1, Pallas kernels, attend(): pl.pallas_call(attend_kernel, grid=(PAIRS,), in_specs=[part(0), part(1),...  42.7 us
    pallas_call x1, Pallas kernels, project_back(): pl.pallas_call(project_back_kernel, out_shape=(sds((hid, D, 3 * D // hid)...  20.1 us
    pallas_call x1, Pallas kernels, project(): pl.pallas_call(project_kernel, out_shape=(jax.ShapeDtypeStruct((D, SEQ),...  16.1 us
    select_n x1, other arithmetic, position_table(): return jnp.where(rows[:, None] < half, jnp.sin(angles), jnp.cos(angles))  12.6 us

profile of v2, /device:TPU:0, one launch (start us, length us, event | category | flops | bytes accessed | tf_op | source)
XLA Modules:
  0.0 451.7 jit_solution(15521308600500877998)
XLA Ops:
  0.6 0.0 copy-start
  0.7 0.9 copy-done
  1.6 0.2 copy.43
  1.8 0.8 copy.45.w1_ref
  2.6 1.4 constant_dynamic-slice_fusion.4.w2_ref
  4.0 0.8 slice_bitcast_fusion.2
  4.8 0.7 stack.32
  5.4 0.7 stack.33
  6.1 0.1 copy.44
  6.2 0.7 pad.11.cols_ref
  6.9 0.7 pad_convert_fusion
  7.6 0.7 reshape.121
  8.3 0.1 pad.25.clone
  8.3 0.7 maximum_maximum_fusion.rows_ref
  9.0 116.8 %gather.1 = (bf16[768,1024]{1,0:T(8,128)(2,1)}, bf16[768,1024]{1,0:T(8,128)(2,1)}, bf16[4,4,2,96,576]{4,3,2,1,0:T(8,128)(2,1)}, bf16[4,4,2,96,192]{4,3,2,1,0:T(8...) custom-call(bf16[192,4096]{1,0:T(8,128)(2,1)} %x_ref.1, ...), custom_call_target="tpu_custom_call" | custom-call | tf_op jit(solution)/shard_map/gather/pallas_call | solution.py:536
  125.8 0.8 slice_bitcast_fusion.1
  126.6 0.1 squeeze.18
  126.7 0.1 squeeze.19
  126.8 0.6 broadcast_in_dim.41.wb_ref
  127.4 0.7 dynamic-slice_convert_fusion
  128.1 12.6 %fusion.tab_ref = f32[768,1024]{1,0:T(8,128)} fusion(f32[1024]{0:T(1024)S(1)} %dynamic-slice_convert_fusion, f32[768]{0:T(1024)S(1)} %fusion.3, pred[768]{0:T(1024)(128)(4,1)S(1)} %iota_compare_fusion), kind=kLoop, calls=%fused_computation.2 | loop fusion | flops 1572864 | bytes 3153664 | tf_op jit(solution)/shard_map/jit(_where)/select_n | solution.py:391
  140.7 16.1 %project.1 = (f32[768,1024]{1,0:T(8,128)}, bf16[768,1024]{1,0:T(8,128)(2,1)}, bf16[1024,2304]{1,0:T(8,128)(2,1)}, bf16[768,2304]{1,0:T(8,128)(2,1)}) custom-call(bf16[768,1024]{1,0:T(8,128)(2,1)} %get-tuple-element.49.x_ref, f32[768,1024]{1,0:T(8,128)} %fusion.tab_ref, f32[768,128]{1,0:T(8,128)} %get-tuple-element.50.p_ref, bf16[4,768,576]{2,1,0:T(8,128)(2,1)} %bitcast.47, ...), custom_call_target="tpu_custom_call" | custom-call | tf_op jit(solution)/shard_map/project/pallas_call | solution.py:84
  156.8 0.0 copy-done.11
  156.8 1.0 copy.46.key_ref
  157.8 42.7 %attend.1 = (bf16[768,1024]{1,0:T(8,128)(2,1)}, f32[6,8,1024]{2,1,0:T(8,128)}) custom-call(bf16[1024,2304]{1,0:T(8,128)(2,1)} %get-tuple-element.53.q_ref.k_ref.v_ref, bf16[1024,2304]{1,0:T(8,128)(2,1)} %get-tuple-element.53.q_ref.k_ref.v_ref, bf16[1024,2304]{1,0:T(8,128)(2,1)} %get-tuple-element.53.q_ref.k_ref.v_ref, s32[1024,1]{1,0:T(8,128)} %copy.46.key_ref, ...), custom_call_target="tpu_custom_call" | custom-call | tf_op jit(solution)/shard_map/attend/pallas_call | solution.py:138
  200.5 1.5 slice.69
  202.0 61.3 %feed.1 = (bf16[768,1024]{1,0:T(8,128)(2,1)}, f32[768,1024]{1,0:T(8,128)}, bf16[1024,768]{1,0:T(8,128)(2,1)}, bf16[768,3072]{1,0:T(8,128)(2,1)}, bf16[768,3072]{...) custom-call(bf16[768,1024]{1,0:T(8,128)(2,1)} %get-tuple-element.54., ...), custom_call_target="tpu_custom_call" | custom-call | tf_op jit(solution)/shard_map/feed/pallas_call | solution.py:243
  263.4 48.1 %attend_back.1 = (bf16[768,1024]{1,0:T(8,128)(2,1)}, bf16[1024,768]{1,0:T(8,128)(2,1)}, bf16[1024,768]{1,0:T(8,128)(2,1)}) custom-call(bf16[1024,2304]{1,0:T(8,128)(2,1)} %get-tuple-element.53.q_ref.k_ref.v_ref, bf16[1024,2304]{1,0:T(8,128)(2,1)} %get-tuple-element.53.q_ref.k_ref.v_ref, bf16[1024,2304]{1,0:T(8,128)(2,1)} %get-tuple-element.53.q_ref.k_ref.v_ref, ...), custom_call_target="tpu_custom_call" | custom-call | tf_op jit(solution)/shard_map/attend_back/pallas_call | solution.py:303
  311.5 20.1 %project_back.1 = (bf16[4,768,576]{2,1,0:T(8,128)(2,1)}, bf16[768,1024]{1,0:T(8,128)(2,1)}, f32[2,8,768]{2,1,0:T(8,128)}, f32[2,768,128]{2,1,0:T(8,128)}) custom-call(bf16[768,1024]{1,0:T(8,128)(2,1)} %get-tuple-element.61.ft_ref, bf16[768,1024]{1,0:T(8,128)(2,1)} %get-tuple-element.64.dqt_ref, bf16[1024,768]{1,0:T(8,128)(2,1)} %get-tuple-element.65.dk_ref, ...), custom_call_target="tpu_custom_call" | custom-call | tf_op jit(solution)/shard_map/project_back/pallas_call | solution.py:375
  331.5 1.4 reduce_sum.18
  333.0 0.3 reduce_sum.19
  333.3 0.8 slice_reduce_fusion.1
  334.1 0.8 slice_reduce_fusion
  335.0 0.6 maximum_bitcast_fusion.vec_ref
  335.6 105.6 %scatter.1 = (bf16[192,4096]{1,0:T(8,128)(2,1)}, bf16[192,4096]{1,0:T(8,128)(2,1)}, f32[96,576]{1,0:T(8,128)}, f32[96,192]{1,0:T(8,128)}, f32[96,768]{1,0:T(8,12...) custom-call(bf16[768,1024]{1,0:T(8,128)(2,1)} %get-tuple-element.60.o_ref, bf16[768,1024]{1,0:T(8,128)(2,1)} %get-tuple-element.69.x_ref, ...), custom_call_target="tpu_custom_call" | custom-call | tf_op jit(solution)/shard_map/scatter/pallas_call | solution.py:711
  441.3 0.0 copy-start.1
  441.3 3.6 convert_element_type.23
  444.9 0.1 copy.49
  445.0 0.9 copy.50
  445.9 0.6 constant_dynamic-slice_fusion.3
  446.6 0.7 dynamic_slice.27
  447.2 0.1 constant_dynamic-slice_fusion.1
  447.3 0.5 slice_bitcast_fusion.6
  447.8 0.6 constant_dynamic-slice_fusion.2
  448.5 1.1 copy.58
  449.6 0.6 copy.59
  450.3 0.7 copy.60
  451.0 0.7 copy.61
  (38 shorter events, 0.2 us)
Async XLA Ops:
  0.6 1.0 copy-start
  140.7 16.2 %copy-start.9 = (s32[1024]{0:T(1024)S(1)}, s32[1024]{0:T(1024)}, u32[]{:S(2)}) copy-start(s32[1024]{0:T(1024)} %param.17) | copy-start | bytes 12292
  140.7 16.2 %copy-start.11 = (s32[1024]{0:T(1024)S(1)}, s32[1024]{0:T(1024)}, u32[]{:S(2)}) copy-start(s32[1024]{0:T(1024)} %param.18) | copy-start | bytes 12292
  311.5 21.5 %copy-start.3 = (f32[2,768,128]{2,1,0:T(8,128)S(1)}, f32[2,768,128]{2,1,0:T(8,128)}, u32[]{:S(2)}) copy-start(f32[2,768,128]{2,1,0:T(8,128)} %get-tuple-element.75) | copy-start | bytes 2359300
  311.5 23.5 %copy-start.10 = (f32[1,3072]{1,0:T(1,128)S(1)}, f32[1,3072]{1,0:T(1,128)}, u32[]{:S(2)}) copy-start(f32[1,3072]{1,0:T(1,128)} %get-tuple-element.78) | copy-start | bytes 36868
  441.2 3.6 copy-start.6
  441.2 4.7 %copy-start.8 = (f32[72,128]{1,0:T(8,128)S(1)}, f32[72,128]{1,0:T(8,128)}, u32[]{:S(2)}) copy-start(f32[72,128]{1,0:T(8,128)} %get-tuple-element.81) | copy-start | bytes 110596
  441.2 7.2 %copy-start.2 = (bf16[192,4096]{1,0:T(8,128)(2,1)S(1)}, bf16[192,4096]{1,0:T(8,128)(2,1)}, u32[]{:S(2)}) copy-start(bf16[192,4096]{1,0:T(8,128)(2,1)} %get-tuple-element.150) | copy-start | bytes 4718596
  441.3 10.4 %copy-start.1 = (bf16[192,3,192]{2,0,1:T(8,128)(2,1)S(1)}, bf16[192,3,192]{2,0,1:T(8,128)(2,1)}, u32[]{:S(2)}) copy-start(bf16[192,3,192]{2,0,1:T(8,128)(2,1)} %param.21) | copy-start | bytes 663556
  444.8 4.8 %copy-start.7 = (f32[96,192]{1,0:T(8,128)S(1)}, f32[96,192]{1,0:T(8,128)}, u32[]{:S(2)}) copy-start(f32[96,192]{1,0:T(8,128)} %get-tuple-element.156) | copy-start | bytes 221188
  444.8 5.4 %copy-start.5 = (f32[96,768]{1,0:T(8,128)S(1)}, f32[96,768]{1,0:T(8,128)}, u32[]{:S(2)}) copy-start(f32[96,768]{1,0:T(8,128)} %get-tuple-element.158) | copy-start | bytes 884740
  444.8 6.1 %copy-start.4 = (f32[96,768]{1,0:T(8,128)S(1)}, f32[96,768]{1,0:T(8,128)}, u32[]{:S(2)}) copy-start(f32[96,768]{1,0:T(8,128)} %get-tuple-element.160) | copy-start | bytes 884740

commit v3 on v1

v3 whole, which is shorter than its diff:
```python
import functools
import math

import jax
import jax.numpy as jnp
from jax import lax
from jax.experimental import pallas as pl
from jax.experimental.pallas import tpu as pltpu
from jax.sharding import PartitionSpec as P

D = 768
HEADS = 12
HD = 64
SEQ = 1024
FB = 256
QB = 256
PAIR = 2 * HD
PAIRS = HEADS // 2
EPS = 1e-06
MASKED = -1e30
F32 = jnp.float32
BF16 = jnp.bfloat16
VMEM_LIMIT = 60 * 1024 * 1024
PI_2 = (1.5703125, 4.837512969970703125e-4, 7.549789948768648e-8)

NN = (((1,), (0,)), ((), ()))
NT = (((1,), (1,)), ((), ()))


def mm(a, b, dims=NN):
    return lax.dot_general(a, b, dims, preferred_element_type=F32)


def whole(shape):
    return pl.BlockSpec(shape, lambda *_: (0,) * len(shape), pipeline_mode=pl.Buffered(1))


def params(**kw):
    return pltpu.CompilerParams(vmem_limit_bytes=VMEM_LIMIT, **kw)


def lane_sums(x):
    total = x[:, 0:128]
    for j in range(1, x.shape[1] // 128):
        total = total + x[:, j * 128 : (j + 1) * 128]
    return total


def norm_stats(e):
    average = jnp.sum(e, axis=0, keepdims=True) * (1.0 / D)
    spread = jnp.sum(e * e, axis=0, keepdims=True) * (1.0 / D) - average * average
    return average, lax.rsqrt(spread + EPS)


def fill_bias(bias_ref, key_ref, seg_ref):
    def rows_of(i, _):
        rows = pl.ds(pl.multiple_of(i * 256, 256), 256)
        same = key_ref[rows, :] == seg_ref[...]
        row_id = lax.broadcasted_iota(jnp.int32, (256, SEQ), 0) + i * 256
        col_id = lax.broadcasted_iota(jnp.int32, (256, SEQ), 1)
        bias_ref[rows, :] = jnp.where(same | (row_id == col_id), 0.0, MASKED)
        return 0

    lax.fori_loop(0, SEQ // 256, rows_of, 0)


MESH = pl.DeviceIdType.MESH


class Wire:
    def __init__(self, send, recv):
        self.send_sem, self.recv_sem, self.count, self.sent = send, recv, 0, []
        self.me = (lax.axis_index("dp"), lax.axis_index("mp"), lax.axis_index("hidden"))
        self.size = (lax.axis_size("dp"), lax.axis_size("mp"), lax.axis_size("hidden"))

    def peer(self, axis, offset):
        where = list(self.me)
        where[axis] = lax.rem(where[axis] + offset, self.size[axis])
        return tuple(where)

    def origin(self, axis, offset):
        return lax.rem(self.me[axis] - offset + self.size[axis], self.size[axis])

    def meet(self):
        barrier = pltpu.get_barrier_semaphore()
        total = 0
        for axis in range(3):
            for offset in range(1, self.size[axis]):
                pl.semaphore_signal(barrier, 1, device_id=self.peer(axis, offset), device_id_type=MESH)
                total += 1
        pl.semaphore_wait(barrier, total)

    def send(self, src, dst, target):
        copy = pltpu.make_async_remote_copy(
            src, dst, self.send_sem.at[self.count], self.recv_sem.at[self.count], device_id=target, device_id_type=MESH
        )
        copy.start()
        self.count += 1
        self.sent.append(copy)
        return copy

    def keep(self, src, dst):
        copy = pltpu.make_async_copy(src, dst, self.send_sem.at[self.count])
        copy.start()
        self.count += 1
        return copy

    def finish(self):
        for copy in self.sent:
            copy.wait_send()


DP, MP, HID = 0, 1, 2


HALF = D // 2


def sin_cos(angles):
    turns = jnp.floor(angles * (2.0 / math.pi) + 0.5)
    r = ((angles - turns * PI_2[0]) - turns * PI_2[1]) - turns * PI_2[2]
    r2 = r * r
    s = r + r * r2 * (-1.6666654611e-1 + r2 * (8.3321608736e-3 + r2 * -1.9515295891e-4))
    c = 1.0 - 0.5 * r2 + r2 * r2 * (4.166664568298827e-2 + r2 * (-1.388731625493765e-3 + r2 * 2.443315711809948e-5))
    quarter = turns - 4.0 * jnp.floor(turns * 0.25)
    odd = (quarter == 1.0) | (quarter == 3.0)
    flip_s = quarter >= 2.0
    flip_c = (quarter == 1.0) | (quarter == 2.0)
    sine = jnp.where(odd, c, s)
    cosine = jnp.where(odd, s, c)
    return jnp.where(flip_s, -sine, sine), jnp.where(flip_c, -cosine, cosine)


def forward_kernel(
    x_ref, c_ref, w1a_ref, w1b_ref, w2_ref, we_ref, wr_ref, cols_ref, rows_ref, pos_ref, rate_ref, key_ref, seg_ref,
    et_out, ft_out, w1_out, qkv_out, at_ref, lse_ref, ct_ref, w2f_ref, wef_ref, wrf_ref, p_ref, rowsf_ref,
    xt, w1af, w1bf, tab, et, ft, f, w1, qkv, bias, vt, wb, send, recv,
):
    wire = Wire(send, recv)
    d, m, h = wire.me
    dp, mp, hid = wire.size
    rows = D // mp
    wide = D // hid
    fcols = we_ref.shape[1]
    half = rows // dp
    offset = pl.multiple_of(d * half, half)
    hs = lambda hh: pl.ds(pl.multiple_of(hh * fcols, fcols), fcols)
    own = (
        (w1a_ref, lambda mm_, hh: w1af.at[hh, mm_, d], lambda: w1af.at[:, :, d], HID),
        (w1b_ref, lambda mm_, hh: w1bf.at[hh, mm_, d], lambda: w1bf.at[:, :, d], MP),
        (w2_ref, lambda mm_, hh: w2f_ref.at[mm_, hh, d], lambda: w2f_ref.at[:, :, d], HID),
        (we_ref.at[pl.ds(offset, half)], lambda mm_, hh: wef_ref.at[mm_, d, :, hs(hh)], lambda: wef_ref.at[:, d], HID),
        (wr_ref.at[pl.ds(offset, half)], lambda mm_, hh: wrf_ref.at[mm_, d, :, hs(hh)], lambda: wrf_ref.at[:, d], MP),
    )
    wire.meet()
    waits, stored = [], []
    first, second, third = {}, {}, {}

    def swap(src_ref, dst_ref):
        mine = pl.ds(pl.multiple_of(m * rows, rows), rows)
        moved = []
        for q in range(1, mp):
            to = wire.peer(MP, q)
            moved.append(wire.send(src_ref.at[:, pl.ds(pl.multiple_of(to[1] * SEQ, SEQ), SEQ)], dst_ref.at[mine], to))
        return moved, wire.keep(src_ref.at[:, pl.ds(pl.multiple_of(m * SEQ, SEQ), SEQ)], dst_ref.at[mine])

    def landed(pair):
        for copy in pair[0]:
            copy.wait_recv()
        pair[1].wait()

    def stage_one(i):
        src, dst, _, axis = own[i]
        first[i] = [wire.keep(src, dst(m, h))]
        first[i] += [wire.send(src, dst(m, h), wire.peer(axis, o)) for o in range(1, wire.size[axis])]

    def stage_two(i):
        _, dst, _, axis = own[i]
        other = MP if axis == HID else HID
        second[i] = []
        for o, copy in enumerate(first[i]):
            if o == 0:
                copy.wait()
            else:
                copy.wait_recv()
            at = wire.origin(axis, o)
            piece = dst(m, at) if axis == HID else dst(at, h)
            second[i] += [wire.send(piece, piece, wire.peer(other, q)) for q in range(1, wire.size[other])]

    def stage_three(i):
        for copy in second[i]:
            copy.wait_recv()
        third[i] = [wire.send(own[i][2](), own[i][2](), wire.peer(DP, r)) for r in range(1, dp)]

    def done(i):
        for copy in third[i]:
            copy.wait_recv()

    mine = pl.ds(pl.multiple_of(m * rows, rows), rows)
    small = [wire.send(cols_ref, p_ref.at[mine], wire.peer(MP, q)) for q in range(1, mp)]
    small += [wire.send(rows_ref, rowsf_ref.at[h], wire.peer(HID, o)) for o in range(1, hid)]
    kept = [wire.keep(cols_ref, p_ref.at[mine]), wire.keep(rows_ref, rowsf_ref.at[h])]
    stage_one(0)
    stage_one(1)
    x_in = swap(x_ref, xt)

    def table_rows(j, _):
        at = pl.ds(pl.multiple_of(j * 64, 64), 64)
        sine, cosine = sin_cos(rate_ref[at, :] * pos_ref[...])
        tab[at, :] = sine
        tab[pl.ds(pl.multiple_of(j * 64 + HALF, 64), 64), :] = cosine
        return 0

    lax.fori_loop(0, 2, table_rows, 0)
    stage_two(0)
    stage_two(1)
    for i in (2, 3, 4):
        stage_one(i)
    lax.fori_loop(2, HALF // 64, table_rows, 0)
    fill_bias(bias, key_ref, seg_ref)
    c_in = swap(c_ref, ct_ref)
    for copy in small:
        copy.wait_recv()
    for copy in kept:
        copy.wait()
    wb[...] = jnp.zeros_like(wb)
    for hh in range(hid):
        wb[:, hh * wide : (hh + 1) * wide] = rowsf_ref[hh, 1:2, :wide]
        wb[:, 2 * D + hh * wide : 2 * D + (hh + 1) * wide] = rowsf_ref[hh, 2:3, :wide]
    landed(x_in)

    def norm_cols(j, _):
        cols = pl.ds(pl.multiple_of(j * 256, 256), 256)
        e = xt[:, cols].astype(F32) + tab[:, cols]
        et[:, cols] = e
        average, inv = norm_stats(e)
        low = ((e - average) * inv * p_ref[:, 0:1] + p_ref[:, 1:2]).astype(BF16)
        ft[:, cols] = low
        f[cols, :] = low.T
        return 0

    lax.fori_loop(0, SEQ // 256, norm_cols, 0)
    stored += [wire.keep(et, et_out), wire.keep(ft, ft_out)]
    stage_three(0)
    stage_three(1)
    stage_two(2)
    done(0)
    done(1)
    for hh in range(hid):
        for mm_ in range(mp):
            for dd in range(dp):
                at = slice(mm_ * rows + dd * half, mm_ * rows + (dd + 1) * half)
                for k in range(3):
                    if k < 2:
                        part = w1af[hh, mm_, dd, :, k * wide : (k + 1) * wide]
                    else:
                        part = w1bf[hh, mm_, dd]
                    w1[at, k * D + hh * wide : k * D + (hh + 1) * wide] = part
    stored.append(wire.keep(w1, w1_out))

    def cols_of(n, scale):
        cols = pl.ds(pl.multiple_of(n * 256, 256), 256)
        y = (mm(f[...], w1[:, cols]) + wb[:, cols]).astype(BF16)
        qkv[:, cols] = y * jnp.asarray(scale, BF16)
        return 0

    lax.fori_loop(0, D // 256, lambda n, c: cols_of(n, HD**-0.5), 0)
    stage_two(3)
    lax.fori_loop(D // 256, 3 * D // 256, lambda n, c: cols_of(n, 1.0), 0)
    stored.append(wire.keep(qkv, qkv_out))
    stage_two(4)

    low = lax.broadcasted_iota(jnp.int32, (QB, PAIR), 1) < HD
    lse_ref[...] = jnp.zeros_like(lse_ref)

    def pair_of(p, _):
        lanes = pl.ds(pl.multiple_of(p * PAIR, PAIR), PAIR)
        k_lanes = pl.ds(pl.multiple_of(p * PAIR + D, PAIR), PAIR)
        v_lanes = pl.ds(pl.multiple_of(p * PAIR + 2 * D, PAIR), PAIR)
        vt[...] = qkv[:, v_lanes].T

        def block(j, _):
            cols = pl.ds(pl.multiple_of(j * QB, QB), QB)
            q = qkv[cols, lanes]
            for hh in range(2):
                qm = jnp.where(low if hh == 0 else ~low, q, jnp.zeros_like(q))
                s = mm(qkv[:, k_lanes], qm, NT) + bias[:, cols]
                top = jnp.max(s, axis=0, keepdims=True)
                e = jnp.exp(s - top)
                total = jnp.sum(e, axis=0, keepdims=True)
                o = mm(vt[hh * HD : (hh + 1) * HD, :], e.astype(BF16)) / total
                at_ref[pl.ds(pl.multiple_of(p * PAIR + hh * HD, HD), HD), cols] = o.astype(BF16)
                lse_ref[p, hh : hh + 1, cols] = top + jnp.log(total)
            return 0

        lax.fori_loop(0, SEQ // QB, block, 0)
        return 0

    lax.fori_loop(0, 2, pair_of, 0)
    stage_three(2)
    lax.fori_loop(2, 4, pair_of, 0)
    stage_three(3)
    lax.fori_loop(4, PAIRS, pair_of, 0)
    stage_three(4)
    landed(c_in)
    for i in (2, 3, 4):
        done(i)
    for copy in stored:
        copy.wait()
    wire.finish()


def forward(x, c, w1a, w1b, w2, we, wr, cols, rows, pos, rate, key_col, seg_row):
    dp, mp, hid = lax.axis_size("dp"), lax.axis_size("mp"), lax.axis_size("hidden")
    half = D // mp // dp
    ff = hid * we.shape[1]
    sds = jax.ShapeDtypeStruct
    out_shape = (
        sds((D, SEQ), F32), sds((D, SEQ), BF16), sds((D, 3 * D), BF16), sds((SEQ, 3 * D), BF16),
        sds((D, SEQ), BF16), sds((PAIRS, 8, SEQ), F32),
        sds((D, SEQ), BF16), sds((mp, hid, dp) + w2.shape, BF16), sds((mp, dp, half, ff), BF16),
        sds((mp, dp, half, ff), BF16), sds((D, cols.shape[1]), F32), sds((hid,) + rows.shape, F32),
    )
    n = 3 * mp + hid + 5 * (hid + mp + hid * mp + dp) + 16
    hbm = pl.BlockSpec(memory_space=pl.ANY)
    vmem = pl.BlockSpec(memory_space=pltpu.VMEM)
    vm = lambda dtype, *shape: pltpu.VMEM(shape, dtype)
    return pl.pallas_call(
        forward_kernel,
        out_shape=out_shape,
        in_specs=[hbm] * 9 + [vmem] * 4,
        out_specs=(hbm,) * 4 + (vmem,) * 2 + (hbm,) * 4 + (vmem,) * 2,
        scratch_shapes=[
            vm(BF16, D, SEQ), vm(BF16, hid, mp, dp, half, w1a.shape[1]), vm(BF16, hid, mp, dp, half, w1b.shape[1]),
            vm(F32, D, SEQ), vm(F32, D, SEQ), vm(BF16, D, SEQ), vm(BF16, SEQ, D), vm(BF16, D, 3 * D),
            vm(BF16, SEQ, 3 * D), vm(F32, SEQ, SEQ), vm(BF16, PAIR, SEQ), vm(F32, 1, 3 * D),
            pltpu.SemaphoreType.DMA((n,)), pltpu.SemaphoreType.DMA((n,)),
        ],
        compiler_params=params(collective_id=0, has_side_effects=True),
        name="forward",
    )(x, c, w1a, w1b, w2, we, wr, cols, rows, pos, rate, key_col, seg_row)


def feed_kernel(
    at_ref, et_ref, ct_ref, w2n_ref, p_ref, we_ref, be_ref, wr_ref,
    out_ref, dmid_ref, do_ref, dwr_ref, dwe_ref, dbe_ref, dw2_ref, db_ref, dg_ref,
    s_ref, st_ref, c_ref, ot_ref, ds_ref, mid_ref, bt_ref, w2_ref,
):
    step = pl.program_id(0)

    @pl.when(step == 0)
    def _():
        mp = w2n_ref.shape[0]
        wide = D // mp
        for j in range(mp):
            w2_ref[:, j * wide : (j + 1) * wide] = w2n_ref[j]
        w2t = w2_ref[...].T

        def cols_of(j, _):
            cols = pl.ds(pl.multiple_of(j * 256, 256), 256)
            mid = et_ref[:, cols] + (mm(w2t, at_ref[:, cols]) + p_ref[:, 4:5])
            mid_ref[:, cols] = mid
            average, inv = norm_stats(mid)
            s = ((mid - average) * inv * p_ref[:, 2:3] + p_ref[:, 3:4]).astype(BF16)
            st_ref[:, cols] = s
            s_ref[cols, :] = s.T
            c_ref[cols, :] = ct_ref[:, cols].T
            return 0

        lax.fori_loop(0, SEQ // 256, cols_of, 0)

    pre = mm(s_ref[...], we_ref[...]) + be_ref[...]
    cdf = 0.5 * (1.0 + lax.erf(pre * (1.0 / math.sqrt(2.0))))
    act = (pre * cdf).astype(BF16)
    slope = cdf + pre * jnp.exp(-0.5 * pre * pre) * (1.0 / math.sqrt(2.0 * math.pi))
    grad = (mm(c_ref[...], wr_ref[...]) * slope).astype(BF16)
    dwr_ref[...] = mm(ct_ref[...], act).astype(BF16)
    dwe_ref[...] = mm(st_ref[...], grad).astype(BF16)
    dbe_ref[...] = jnp.sum(grad.astype(F32), axis=0, keepdims=True)
    o = mm(wr_ref[...], act, NT)
    ds = mm(we_ref[...], grad, NT)

    @pl.when(step == 0)
    def _():
        ot_ref[...] = o
        ds_ref[...] = ds

    @pl.when(step > 0)
    def _():
        ot_ref[...] += o
        ds_ref[...] += ds

    @pl.when(step == pl.num_programs(0) - 1)
    def _():
        dg_ref[...] = jnp.zeros_like(dg_ref)

        def cols_of(j, _):
            cols = pl.ds(pl.multiple_of(j * 256, 256), 256)
            mid = mid_ref[:, cols]
            out_ref[:, cols] = (mid + (ot_ref[:, cols] + p_ref[:, 5:6])).astype(BF16)
            average, inv = norm_stats(mid)
            normed = (mid - average) * inv
            ds = ds_ref[:, cols]
            scaled = ds * p_ref[:, 2:3]
            total = jnp.sum(scaled, axis=0, keepdims=True) * (1.0 / D)
            crossed = jnp.sum(scaled * normed, axis=0, keepdims=True) * (1.0 / D)
            dmid = ct_ref[:, cols].astype(F32) + inv * (scaled - total - normed * crossed)
            dmid_ref[:, cols] = dmid
            low = dmid.astype(BF16)
            bt_ref[:, cols] = low
            do_ref[cols, :] = mm(w2_ref[...], low).astype(BF16).T
            dg_ref[0] += lane_sums(ds * normed)
            dg_ref[1] += lane_sums(ds)
            return 0

        lax.fori_loop(0, SEQ // 256, cols_of, 0)
        ones = jnp.ones((8, SEQ), BF16)
        db_ref[0] = mm(ones, ct_ref[...], NT)
        db_ref[1] = mm(ones, bt_ref[...], NT)

        wide = D // dw2_ref.shape[0]
        for j in range(dw2_ref.shape[0]):
            dw2_ref[j] = mm(at_ref[...], bt_ref[j * wide : (j + 1) * wide, :], NT).astype(BF16)


def feed(at, et, ct, w2, small, we, be, wr):
    ff = we.shape[1]
    cols = pl.BlockSpec((D, FB), lambda f: (0, f))
    row = pl.BlockSpec((1, FB), lambda f: (0, f))
    sds = jax.ShapeDtypeStruct
    return pl.pallas_call(
        feed_kernel,
        grid=(ff // FB,),
        in_specs=[
            whole((D, SEQ)), whole((D, SEQ)), whole((D, SEQ)), whole(w2.shape), whole((D, 128)), cols, row, cols,
        ],
        out_specs=(
            whole((D, SEQ)), whole((D, SEQ)), whole((SEQ, D)), cols, cols, row, whole(w2.shape),
            whole((2, 8, D)), whole((2, D, 128)),
        ),
        out_shape=(
            sds((D, SEQ), BF16), sds((D, SEQ), F32), sds((SEQ, D), BF16), sds((D, ff), BF16), sds((D, ff), BF16),
            sds((1, ff), F32), sds(w2.shape, BF16), sds((2, 8, D), F32), sds((2, D, 128), F32),
        ),
        scratch_shapes=[
            pltpu.VMEM((SEQ, D), BF16), pltpu.VMEM((D, SEQ), BF16), pltpu.VMEM((SEQ, D), BF16),
            pltpu.VMEM((D, SEQ), F32), pltpu.VMEM((D, SEQ), F32), pltpu.VMEM((D, SEQ), F32),
            pltpu.VMEM((D, SEQ), BF16), pltpu.VMEM((D, D), BF16),
        ],
        compiler_params=params(),
        name="feed",
    )(at, et, ct, w2, small, we, be, wr)


def backward_kernel(
    o_ref, dw2_ref, dwe_ref, dwr_ref, qkv_in, do_in, lse_ref, key_ref, seg_ref, ft_in, w_in, et_in, dmid_in, p_ref,
    dbe_ref, dbf_ref, dgs_ref,
    of_ref, xf_ref, ga_ref, gb_ref, g2_ref, ge_ref, gr_ref, vecf_ref,
    qkv, do, bias, kt, dqt, dk, dv, dka, dva, ft, w1, et, dmid, dgp,
    a0, a1, a2, a3, a4, o0, o1, s2, s3, s4, b0, b1, b2, b3, b4, t0, t1, t2, t3, t4, c0, c1, c2, c3, c4,
    v0, va, vb, vc, v1, v2, loads, send, recv,
):
    wire = Wire(send, recv)
    d, m, h = wire.me
    dp, mp, hid = wire.size
    rows = D // mp
    wide = D // hid
    half = rows // dp
    fcols = ge_ref.shape[1]
    v_in = (va, vb, vc)
    hslice = lambda hh: pl.ds(pl.multiple_of(hh * fcols, fcols), fcols)

    def load(n, src, dst):
        copy = pltpu.make_async_copy(src, dst, loads.at[n])
        copy.start()
        return copy

    parts = []
    for p in range(PAIRS):
        got = []
        for k in range(3):
            lanes = slice(k * D + p * PAIR, k * D + (p + 1) * PAIR)
            got.append(load(4 * p + k, qkv_in.at[:, lanes], qkv.at[:, lanes]))
        lanes = slice(p * PAIR, (p + 1) * PAIR)
        got.append(load(4 * p + 3, do_in.at[:, lanes], do.at[:, lanes]))
        parts.append(got)
    others = [load(4 * PAIRS + i, a, b) for i, (a, b) in enumerate(((ft_in, ft), (w_in, w1), (et_in, et), (dmid_in, dmid)))]
    wire.meet()
    items = (
        (lambda dd: o0.at[dd], a0, o0.at[d], b0, t0, c0, ga_ref, MP, HID),
        (lambda dd: o1.at[dd], a1, o1.at[d], b1, t1, c1, gb_ref, HID, HID),
        (lambda dd: dw2_ref.at[:, :, dd], a2, s2, b2, t2, c2, g2_ref, MP, MP),
        (lambda dd: dwe_ref.at[:, dd], a3, s3, b3, t3, c3, ge_ref, MP, None),
        (lambda dd: dwr_ref.at[:, dd], a4, s4, b4, t4, c4, gr_ref, HID, None),
    )
    core, kept, near, far = {}, {}, {}, {}

    def stage_core(i):
        src, a, s = items[i][:3]
        core[i] = [wire.send(src(wire.peer(DP, r)[0]), a.at[r - 1], wire.peer(DP, r)) for r in range(1, dp)]
        if i > 1:
            kept[i] = wire.keep(src(d), s)

    def add_all(dst, own, others, shape):
        lead = shape[:-2]

        def body(n, _):
            index = []
            for size in reversed(lead):
                index.insert(0, lax.rem(n, size))
                n = lax.div(n, size)
            index = tuple(index)
            value = own[index].astype(F32)
            for j in range(others.shape[0]):
                value = value + others[(j,) + index].astype(F32)
            dst[index] = value.astype(dst.dtype)
            return 0

        lax.fori_loop(0, math.prod(lead), body, 0)

    def part(i, ref, axis, at, leads):
        if items[i][8] is None:
            return ref.at[(slice(None),) * len(leads) + (slice(None), hslice(at))] if axis == HID else ref.at[at]
        return ref.at[at] if leads[0] == axis else ref.at[:, at]

    def leads_of(i):
        lead = items[i][8]
        return (MP,) if lead is None else ((HID, MP) if lead == HID else (MP, HID))

    def stage_near(i):
        _, a, s, b, t, c, g, axis, _ = items[i]
        for copy in core[i]:
            copy.wait_recv()
        if i in kept:
            kept[i].wait()
        add_all(s, s, a, s.shape)
        near[i] = [
            wire.send(part(i, s, axis, wire.peer(axis, q)[axis], leads_of(i)), b.at[q - 1], wire.peer(axis, q))
            for q in range(1, wire.size[axis])
        ]

    def stage_far(i):
        _, a, s, b, t, c, g, axis, lead = items[i]
        for copy in near[i]:
            copy.wait_recv()
        add_all(t, part(i, s, axis, wire.me[axis], leads_of(i)), b, t.shape)
        other = MP if axis == HID else HID
        left = tuple(x for x in leads_of(i) if x != axis)
        far[i] = []
        for q in range(1, wire.size[other]):
            to = wire.peer(other, q)
            far[i].append(wire.send(part(i, t, other, to[other], left), c.at[q - 1], to))

    def stage_end(i):
        _, a, s, b, t, c, g, axis, lead = items[i]
        other = MP if axis == HID else HID
        left = tuple(x for x in leads_of(i) if x != axis)
        for copy in far[i]:
            copy.wait_recv()
        value = part(i, t, other, wire.me[other], left)[...].astype(F32)
        for j in range(c.shape[0]):
            value = value + c[j].astype(F32)
        g[...] = value

    moved, held = [], []

    def swap(src_ref, dst_ref):
        mine = pl.ds(pl.multiple_of(m * SEQ, SEQ), SEQ)
        for q in range(1, mp):
            to = wire.peer(MP, q)
            moved.append(wire.send(src_ref.at[pl.ds(pl.multiple_of(to[1] * rows, rows), rows)], dst_ref.at[:, mine], to))
        held.append(wire.keep(src_ref.at[pl.ds(pl.multiple_of(m * rows, rows), rows)], dst_ref.at[:, mine]))

    vec = {}

    def vec_send(axis, src):
        vec[axis] = [wire.send(src, v_in[axis].at[o - 1], wire.peer(axis, o)) for o in range(1, wire.size[axis])]

    def vec_sum(axis, src, dst):
        for copy in vec[axis]:
            copy.wait_recv()
        total = src[...]
        for j in range(wire.size[axis] - 1):
            total = total + v_in[axis][j]
        dst[...] = total

    for i in (4, 3, 2):
        stage_core(i)
    swap(o_ref, of_ref)
    fill_bias(bias, key_ref, seg_ref)
    low = lax.broadcasted_iota(jnp.int32, (QB, PAIR), 1) < HD

    def pair_of(p, _):
        off = pl.multiple_of(p * PAIR, PAIR)
        lanes = pl.ds(off, PAIR)
        k_lanes = pl.ds(pl.multiple_of(off + D, PAIR), PAIR)
        v_lanes = pl.ds(pl.multiple_of(off + 2 * D, PAIR), PAIR)
        kt[...] = qkv[:, k_lanes].T
        dka[...] = jnp.zeros_like(dka)
        dva[...] = jnp.zeros_like(dva)

        def block(j, _):
            cols = pl.ds(pl.multiple_of(j * QB, QB), QB)
            q = qkv[cols, lanes]
            g = do[cols, lanes]
            for hh in range(2):
                keep = low if hh == 0 else ~low
                qm = jnp.where(keep, q, jnp.zeros_like(q))
                gm = jnp.where(keep, g, jnp.zeros_like(g))
                e = jnp.exp(mm(qkv[:, k_lanes], qm, NT) + bias[:, cols] - lse_ref[p, hh : hh + 1, cols])
                t = e * mm(qkv[:, v_lanes], gm, NT)
                ds = (t - e * jnp.sum(t, axis=0, keepdims=True)).astype(BF16)
                dva[...] += mm(e.astype(BF16), gm)
                dka[...] += mm(ds, qm)
                dq = mm(kt[hh * HD : (hh + 1) * HD, :], ds) * HD**-0.5
                dqt[pl.ds(pl.multiple_of(off + hh * HD, HD), HD), cols] = dq.astype(BF16)
            return 0

        lax.fori_loop(0, SEQ // QB, block, 0)
        dk[:, lanes] = dka[...].astype(BF16)
        dv[:, lanes] = dva[...].astype(BF16)
        return 0

    def pairs(first, last):
        for p in range(first, last):
            for copy in parts[p]:
                copy.wait()
        lax.fori_loop(first, last, pair_of, 0)

    pairs(0, 1)
    stage_near(4)
    stage_near(3)
    stage_near(2)
    pairs(1, 5)
    stage_far(3)
    stage_far(2)
    pairs(5, PAIRS)
    stage_far(4)
    for copy in others:
        copy.wait()

    for hh in range(hid):
        for k in range(3):
            if k == 0:
                value = mm(ft[...], dqt[hh * wide : (hh + 1) * wide, :], NT).astype(BF16)
            else:
                value = mm(ft[...], (dk, dv)[k - 1][:, hh * wide : (hh + 1) * wide]).astype(BF16)
            for mm_ in range(mp):
                for dd in range(dp):
                    piece = value[mm_ * rows + dd * half : mm_ * rows + (dd + 1) * half, :]
                    if k < 2:
                        o0[dd, hh, mm_, :, k * wide : (k + 1) * wide] = piece
                    else:
                        o1[dd, hh, mm_] = piece
    stage_core(1)
    stage_core(0)
    df = bias.at[pl.ds(0, D)]
    dx = ft

    def feature_cols(j, _):
        cols = pl.ds(pl.multiple_of(j * 256, 256), 256)
        value = mm(w1[:, 0:D], dqt[:, cols])
        value += mm(w1[:, D : 2 * D], dk[cols, :], NT)
        value += mm(w1[:, 2 * D : 3 * D], dv[cols, :], NT)
        df[:, cols] = value
        return 0

    lax.fori_loop(0, SEQ // 256, feature_cols, 0)
    stage_near(1)
    stage_near(0)
    dgp[...] = jnp.zeros_like(dgp)

    def norm_cols(j, _):
        cols = pl.ds(pl.multiple_of(j * 256, 256), 256)
        e = et[:, cols]
        average, inv = norm_stats(e)
        normed = (e - average) * inv
        g = df[:, cols]
        scaled = g * p_ref[:, 0:1]
        total = jnp.sum(scaled, axis=0, keepdims=True) * (1.0 / D)
        crossed = jnp.sum(scaled * normed, axis=0, keepdims=True) * (1.0 / D)
        dx[:, cols] = (dmid[:, cols] + inv * (scaled - total - normed * crossed)).astype(BF16)
        dgp[0] += lane_sums(g * normed)
        dgp[1] += lane_sums(g)
        return 0

    lax.fori_loop(0, SEQ // 256, norm_cols, 0)
    swap(dx, xf_ref)
    ones = jnp.ones((8, SEQ), BF16)
    v0[...] = jnp.zeros_like(v0)
    for n in range(2):
        v0[n : n + 1, :] = jnp.sum(dgp[n].T, axis=0, keepdims=True)
        v0[2 + n : 3 + n, :] = jnp.sum(dgs_ref[n].T, axis=0, keepdims=True)
        v0[6 + n : 7 + n, :] = dbf_ref[n, 0:1, :]
    v0[4:5, :] = mm(ones, dqt[...], NT)[0:1]
    v0[5:6, :] = mm(ones, dv[...])[0:1]
    for n in range(dbe_ref.shape[1] // D):
        v0[8 + n : 9 + n, :] = dbe_ref[:, n * D : (n + 1) * D]
    vec_send(DP, v0)
    stage_end(3)
    stage_end(2)
    vec_sum(DP, v0, v1)
    vec_send(MP, v1)
    stage_far(1)
    stage_far(0)
    vec_sum(MP, v1, v2)
    vec_send(HID, v2)
    stage_end(4)
    stage_end(1)
    stage_end(0)
    vec_sum(HID, v2, vecf_ref)
    for copy in held:
        copy.wait()
    for copy in moved:
        copy.wait_recv()
    wire.finish()


def backward(o, dw2, dwe, dwr, qkv, do, lse, key_col, seg_row, ft, w1, et, dmid, cols, dbe, dbf, dgs):
    dp, mp, hid = lax.axis_size("dp"), lax.axis_size("mp"), lax.axis_size("hidden")
    sds = jax.ShapeDtypeStruct
    wide = D // hid
    half = D // mp // dp
    half2, c2 = dw2.shape[3:]
    ff = dwe.shape[3]
    fc = ff // hid
    out_shape = (
        sds((D // mp, mp * SEQ), BF16), sds((D // mp, mp * SEQ), BF16), sds((half, 2 * wide), F32),
        sds((half, wide), F32), sds((half2, c2), F32), sds((half, fc), F32), sds((half, fc), F32), sds((16, D), F32),
    )
    vm = lambda *shape: pltpu.VMEM(shape, BF16)
    vf = lambda *shape: pltpu.VMEM(shape, F32)
    slabs = (
        (hid, mp, half, 2 * wide), (hid, mp, half, wide), (mp, hid, half2, c2), (mp, half, ff), (mp, half, ff)
    )
    after = ((hid, half, 2 * wide), (mp, half, wide), (hid, half2, c2), (half, ff), (mp, half, fc))
    ends = ((half, 2 * wide), (half, wide), (half2, c2), (half, fc), (half, fc))
    near = (mp, hid, mp, mp, hid)
    far = (hid, mp, hid, hid, mp)
    scratch = [
        vm(SEQ, 3 * D), vm(SEQ, D), vf(SEQ, SEQ), vm(PAIR, SEQ), vm(D, SEQ), vm(SEQ, D), vm(SEQ, D),
        vf(SEQ, PAIR), vf(SEQ, PAIR), vm(D, SEQ), vm(D, 3 * D), vf(D, SEQ), vf(D, SEQ), vf(2, D, 128),
    ]
    scratch += [vm(dp - 1, *s) for s in slabs]
    scratch += [vm(dp, *s) for s in slabs[:2]] + [vm(*s) for s in slabs[2:]]
    scratch += [vm(n - 1, *s) for n, s in zip(near, after)] + [vm(*s) for s in after]
    scratch += [vm(n - 1, *s) for n, s in zip(far, ends)]
    scratch += [vf(16, D), vf(dp - 1, 16, D), vf(mp - 1, 16, D), vf(hid - 1, 16, D), vf(16, D), vf(16, D)]
    n = dp + mp + hid + 2 * mp + 5 * (dp + mp + hid + 1) + 8
    scratch += [pltpu.SemaphoreType.DMA((4 * PAIRS + 4,)), pltpu.SemaphoreType.DMA((n,)), pltpu.SemaphoreType.DMA((n,))]
    hbm = pl.BlockSpec(memory_space=pl.ANY)
    vmem = pl.BlockSpec(memory_space=pltpu.VMEM)
    return pl.pallas_call(
        backward_kernel,
        out_shape=out_shape,
        in_specs=[hbm] * 6 + [vmem] * 3 + [hbm] * 4 + [vmem] * 4,
        out_specs=(hbm, hbm) + (vmem,) * 6,
        scratch_shapes=scratch,
        compiler_params=params(collective_id=1, has_side_effects=True),
        name="backward",
    )(o, dw2, dwe, dwr, qkv, do, lse, key_col, seg_row, ft, w1, et, dmid, cols, dbe, dbf, dgs)


def local(
    stored, positions, segments, present, norm_gains, norm_biases, input_proj, input_bias, output_proj,
    output_bias, expand_weight, expand_bias, reduce_weight, reduce_bias, cotangent,
):
    mp, hid, dp = lax.axis_size("mp"), lax.axis_size("hidden"), lax.axis_size("dp")
    m, h, d = lax.axis_index("mp"), lax.axis_index("hidden"), lax.axis_index("dp")
    rows_mp, hcols, fcols = D // mp, D // hid, expand_weight.shape[1]
    half = rows_mp // dp
    cols = [norm_gains[0], norm_biases[0], norm_gains[1], norm_biases[1], output_bias.astype(F32), reduce_bias.astype(F32)]
    cols = jnp.pad(jnp.stack(cols, axis=1), ((0, 0), (0, 128 - len(cols))))
    rows = jnp.concatenate(
        [
            expand_bias.astype(F32)[None],
            jnp.pad(input_bias.astype(F32), ((0, 0), (0, fcols - hcols))),
            jnp.zeros((5, fcols), F32),
        ]
    )
    w1 = lax.dynamic_slice_in_dim(input_proj, d * half, half, 0)
    w2 = lax.dynamic_slice_in_dim(output_proj, d * (hcols // dp), hcols // dp, 0)
    pos = lax.dynamic_slice_in_dim(positions, m * SEQ, SEQ).astype(F32)[None]
    rate = jnp.exp(jnp.arange(D // 2, dtype=jnp.int32).astype(F32) * (-math.log(10000.0) / (D // 2)))[:, None]
    key_col = jnp.where(present == 1, segments, -1)[:, None]
    seg_row = segments[None, :]
    et, ft, w1f, qkv, at, lse, ct, w2n, we, wr, cols, rows = forward(
        stored, cotangent, w1[:, :2].reshape(half, 2 * hcols), w1[:, 2], w2, expand_weight, reduce_weight, cols, rows,
        pos, rate, key_col, seg_row,
    )
    w2n = w2n.reshape(mp, D, rows_mp)
    we, wr = we.reshape(D, hid * fcols), wr.reshape(D, hid * fcols)
    be = rows[:, 0].reshape(1, hid * fcols)
    out_t, dmid, do, dwr, dwe, dbe, dw2, dbf, dgs = feed(at, et, ct, w2n, cols, we, be, wr)
    output, d_stored, ga, gb, d_output, d_expand, d_reduce, vec = backward(
        out_t,
        dw2.reshape(mp, hid, dp, hcols // dp, rows_mp),
        dwe.reshape(mp, dp, half, hid * fcols),
        dwr.reshape(mp, dp, half, hid * fcols),
        qkv, do, lse, key_col, seg_row, ft, w1f, et, dmid, cols, dbe, dbf, dgs,
    )
    piece = D // (hid * mp * dp)
    cut = lambda x, at, size: lax.dynamic_slice_in_dim(x, at * size, size, x.ndim - 1)
    dg = cut(vec[:4].reshape(2, 2, D), (m * dp + d) * hid + h, piece)
    db_proj = cut(vec[4:6], h * dp + d, hcols // dp)
    db_feed = cut(vec[6:8], m * dp + d, half)
    dbe = cut(vec[8:].reshape(-1)[: hid * fcols], h * dp + d, fcols // dp)
    d_input = jnp.concatenate([ga.reshape(half, 2, hcols), gb[:, None]], axis=1)
    return (
        output, d_stored.astype(F32), dg[:, 0], dg[:, 1], d_input, db_proj, d_output, db_feed[1], d_expand, dbe, d_reduce,
        db_feed[0],
    )


def solution(mesh):
    placed = (
        P("mp", ("dp", "hidden")),
        P(("dp", "hidden")),
        P(("dp", "hidden", "mp")),
        P(("dp", "hidden", "mp")),
        P(None, "mp"),
        P(None, "mp"),
        P("mp", None, "hidden"),
        P(None, "hidden"),
        P("hidden", "mp"),
        P("mp"),
        P("mp", "hidden"),
        P("hidden"),
        P("mp", "hidden"),
        P("mp"),
        P("mp", ("dp", "hidden")),
    )
    return jax.shard_map(
        local,
        mesh=mesh,
        in_specs=placed,
        out_specs=(
            P("mp", ("dp", "hidden")),
            P("mp", ("dp", "hidden")),
            P(None, ("mp", "dp", "hidden")),
            P(None, ("mp", "dp", "hidden")),
            P(("mp", "dp"), None, "hidden"),
            P(None, ("hidden", "dp")),
            P(("hidden", "dp"), "mp"),
            P(("mp", "dp")),
            P(("mp", "dp"), "hidden"),
            P(("hidden", "dp")),
            P(("mp", "dp"), "hidden"),
            P(("mp", "dp")),
        ),
        check_vma=False,
    )
```

time: 707 us -> 337 us (0.48)
  local copies, waits for them, and re-layouts: 195 us -> 15.8 us
  Pallas kernels: 187 us -> 311 us
  waiting for transfers between devices: 120 us -> 0 us
  blocking collectives: 116 us -> 0 us
  other arithmetic: 48.2 us -> 9.16 us
  starting transfers between devices: 17.8 us -> 0 us
  between operations: 15.3 us -> 0.8 us
    pallas_call x4 -> x2, Pallas kernels: 125 us -> 249 us  [the longest x1 125 us: backward(): pl.pallas_call(backward_kernel, out_shape=out_shape, in_specs=[hbm] * 6 +...]
    reshape x24 -> x4, local copies, waits for them, and re-layouts: 124 us -> 1.86 us  [the longest x2 1.1 us: local(): d_input = jnp.concatenate([ga.reshape(half, 2, hcols), gb[:, None]], axis=1)]
    reduce_scatter x1 -> x0, waiting for transfers between devices: 82.8 us -> none  [local(): lax.psum_scatter(packed, GATHER, scatter_dimension=0, tiled=True)]
    all_gather x4 -> x0, blocking collectives: 57.2 us -> none  [the longest x2 32.6 us: local(): lax.all_gather(t, 'mp', axis=1, tiled=True)]
    psum x1 -> x0, blocking collectives: 49.6 us -> none  [local(): vectors = lax.psum(vectors, ('dp', 'mp', 'hidden'))]
    concatenate x4 -> x2, other arithmetic: 31.7 us -> 2.31 us  [the longest x1 1.63 us: local(): d_input = jnp.concatenate([ga.reshape(half, 2, hcols), gb[:, None]], axis=1)]
    all_to_all x4 -> x0, waiting for transfers between devices: 22.6 us -> none  [the longest x1 22.6 us: local(): lax.all_to_all(out_t, 'mp', split_axis=0, concat_axis=1, tiled=True)]
    transpose x3 -> x0, local copies, waits for them, and re-layouts: 22.2 us -> none  [the longest x1 9.93 us: local(): full[..., :o0].reshape(hid, D, 3, hcols).transpose(1, 2, 0, 3)]
  transfers between devices with their start and end apart: 6 -> 0, of which waited for: 3 -> 0; matrix products, arithmetic and copies ran while one was open for 20% -> 0% of each run, Pallas kernels for 8% -> 0%
where the time goes in v3:
time: 337 us; the launch traced here: 336 us
  Pallas kernels  311 us (92%)
  local copies, waits for them, and re-layouts  15.8 us (5%)
  other arithmetic  9.16 us (3%)
    pallas_call x1, Pallas kernels, backward(): pl.pallas_call(backward_kernel, out_shape=out_shape, in_specs=[hbm] * 6 +...  125 us
    pallas_call x1, Pallas kernels, forward(): pl.pallas_call(forward_kernel, out_shape=out_shape, in_specs=[hbm] * 9 +...  124 us
    pallas_call x1, Pallas kernels, feed(): pl.pallas_call(feed_kernel, grid=(ff // FB,), in_specs=[whole((D, SEQ)),...  61.4 us

profile of v3, /device:TPU:0, one launch (start us, length us, event | category | flops | bytes accessed | tf_op | source)
XLA Modules:
  0.0 336.4 jit_solution(9879194636438815025)
XLA Ops:
  0.6 0.0 copy-start
  0.7 0.0 copy-start.7
  0.7 0.0 copy-start.6
  0.7 0.9 copy-done
  1.6 0.1 copy.46
  1.7 0.7 reshape.66.w1a_ref
  2.5 0.6 dynamic-slice_bitcast_fusion.w1b_ref
  3.1 1.4 constant_dynamic-slice_fusion.5.w2_ref
  4.5 1.3 dynamic-slice_convert_fusion
  5.8 0.8 slice_bitcast_fusion
  6.6 0.7 stack.20
  7.2 0.7 stack.21
  7.9 0.1 copy.47
  8.0 0.7 pad.11.cols_ref
  8.7 0.7 compare_select_fusion
  9.4 1.0 copy.50.key_ref
  10.4 0.1 copy.49
  10.6 0.7 exp.10.rate_ref
  11.3 0.0 copy-done.7
  11.3 0.0 copy-done.6
  11.3 0.1 pad.18.clone
  11.4 0.7 maximum_maximum_fusion.rows_ref
  12.1 124.0 %forward.1 = (f32[768,1024]{1,0:T(8,128)}, bf16[768,1024]{1,0:T(8,128)(2,1)}, bf16[768,2304]{1,0:T(8,128)(2,1)}, bf16[1024,2304]{1,0:T(8,128)(2,1)}, bf16[768,10...) custom-call(bf16[192,4096]{1,0:T(8,128)(2,1)} %x_ref.1, ...), custom_call_target="tpu_custom_call" | custom-call | tf_op jit(solution)/shard_map/forward/pallas_call | solution.py:328
  136.1 1.5 slice.56
  137.6 61.4 %feed.1 = (bf16[768,1024]{1,0:T(8,128)(2,1)}, f32[768,1024]{1,0:T(8,128)}, bf16[1024,768]{1,0:T(8,128)(2,1)}, bf16[768,3072]{1,0:T(8,128)(2,1)}, bf16[768,3072]{...) custom-call(bf16[768,1024]{1,0:T(8,128)(2,1)} %get-tuple-element.41., ...), custom_call_target="tpu_custom_call" | custom-call | tf_op jit(solution)/shard_map/feed/pallas_call | solution.py:431
  199.0 125.3 %backward.1 = (bf16[192,4096]{1,0:T(8,128)(2,1)}, bf16[192,4096]{1,0:T(8,128)(2,1)}, f32[96,384]{1,0:T(8,128)}, f32[96,192]{1,0:T(8,128)}, f32[96,192]{1,0:T(8,1...) custom-call(bf16[768,1024]{1,0:T(8,128)(2,1)} %get-tuple-element.49.o_ref, ...), custom_call_target="tpu_custom_call" | custom-call | tf_op jit(solution)/shard_map/backward/pallas_call | solution.py:753
  324.3 1.1 reshape.74
  325.4 1.6 pad_maximum_fusion
  327.1 0.0 copy-start.5
  327.1 0.0 copy-start.1
  327.1 3.5 %convert_element_type.26 = f32[192,4096]{1,0:T(8,128)} convert(bf16[192,4096]{1,0:T(8,128)(2,1)} %get-tuple-element.63) | non-fusion elementwise | flops 786432 | bytes 4718592 | tf_op jit(solution)/shard_map/convert_element_type | solution.py:810
  330.6 0.0 copy-done.5
  330.6 0.6 constant_dynamic-slice_fusion.4
  331.3 0.7 dynamic_slice.27
  332.0 0.1 constant_dynamic-slice_fusion.2
  332.0 0.5 slice_bitcast_fusion.4
  332.6 0.6 constant_dynamic-slice_fusion.3
  333.2 0.0 copy-done.1
  333.2 0.0 copy-start.4
  333.2 0.0 copy-start.3
  333.2 0.0 copy-start.2
  333.2 1.1 copy.61
  334.4 0.0 copy-done.4
  334.4 0.6 copy.62
  335.0 0.0 copy-done.3
  335.0 0.7 copy.63
  335.7 0.0 copy-done.2
  335.7 0.7 copy.64
  (11 shorter events, 0.1 us)
Async XLA Ops:
  0.6 1.0 copy-start
  0.7 10.6 %copy-start.7 = (bf16[2,192]{1,0:T(2,128)(2,1)S(1)}, bf16[2,192]{1,0:T(2,128)(2,1)}, u32[]{:S(2)}) copy-start(bf16[2,192]{1,0:T(2,128)(2,1)} %param.22) | copy-start | bytes 2308
  0.7 10.6 %copy-start.6 = (bf16[768]{0:T(1024)(128)(2,1)S(1)}, bf16[768]{0:T(1024)(128)(2,1)}, u32[]{:S(2)}) copy-start(bf16[768]{0:T(1024)(128)(2,1)} %param.26) | copy-start | bytes 4612
  327.1 3.6 %copy-start.5 = (f32[16,768]{1,0:T(8,128)S(1)}, f32[16,768]{1,0:T(8,128)}, u32[]{:S(2)}) copy-start(f32[16,768]{1,0:T(8,128)} %get-tuple-element.64) | copy-start | bytes 147460
  327.1 6.1 %copy-start.1 = (bf16[192,4096]{1,0:T(8,128)(2,1)S(1)}, bf16[192,4096]{1,0:T(8,128)(2,1)}, u32[]{:S(2)}) copy-start(bf16[192,4096]{1,0:T(8,128)(2,1)} %get-tuple-element.96) | copy-start | bytes 4718596
  333.2 1.2 copy-start.4
  333.2 1.8 copy-start.3
  333.2 2.5 copy-start.2
